TPU v7x, 32 devices: a whole 2x2x4 slice. The times are simulated.
32 devices in a mesh: seq: 2 (over x), exp: 16 (over z, y, core).
Axes of the slice: x: 2, y: 2, z: 4, core: 2. Of those that a mesh axis runs over, the one named last changes fastest.
Arguments:
- queries: bfloat16 [2048, 64, 576], P('seq', 'exp'), may hold values from -68 to 68
- keys: bfloat16 [2048, 576], P(('seq', 'exp')), may hold values from -4.5 to 4.5
- block_mask: int32 [4, 4, 8], replicated, may hold values from 0 to 1, as said below
- summary_start: int32 [4], replicated, may hold values from 0 to 448, as said below
Outputs:
- context: bfloat16 [2048, 64, 512], P('seq', 'exp')
Inputs may be any that keep to these rules, and one draw needn't show every extreme that they name: block_mask[c, i, i] is 1, entries of own blocks j > i are 0, and entry 4 + c (the candidate's own summary) is 0. `summary_start`: every value is a multiple of 64.
All inputs are finite; a program needn't handle non-finite values.
Results may differ from a plain program's by a relative error of at most 0.0035.
Values may be sent and summed in bfloat16 or wider, within the bound.
No kernel may reach another device: no remote copies, remote signals or barrier semaphores. Data moves between devices by JAX's collectives and lax.ppermute only.
A program may use at most 64 MiB of HBM per device.

v0:
```python
import jax
import jax.numpy as jnp
from jax import lax
from jax.sharding import PartitionSpec as P

ROPE = 64
NBLK = 4
CPG = 2


score_scale = 192.0 ** (-0.5)
neg_big = -1e30


def absorb_keys(carried, query_rows, block_keys, allowed, lat_width):
    running_max, weight_sum, numerator = carried
    scores = (
        jnp.einsum("rhd,kd->rhk", query_rows, block_keys, preferred_element_type=jnp.float32)
        * score_scale
    )
    scores = jnp.where(allowed[:, None, :], scores, neg_big)
    new_max = jnp.maximum(running_max, jnp.max(scores, axis=2))
    factor = jnp.exp(running_max - new_max)
    weights = jnp.where(allowed[:, None, :], jnp.exp(scores - new_max[..., None]), 0.0)
    weight_sum = weight_sum * factor + jnp.sum(weights, axis=2)
    numerator = numerator * factor[..., None] + jnp.einsum(
        "rhk,kd->rhd",
        weights.astype(jnp.bfloat16),
        block_keys[:, :lat_width],
        preferred_element_type=jnp.float32,
    )
    return (new_max, weight_sum, numerator)


def start_state(row_total, head_count, lat_width):
    return (
        jnp.full((row_total, head_count), neg_big, jnp.float32),
        jnp.zeros((row_total, head_count), jnp.float32),
        jnp.zeros((row_total, head_count, lat_width), jnp.float32),
    )


def shards(queries, keys, block_mask, summary_start):
    row_total = queries.shape[0]
    head_count = queries.shape[1]
    key_width = keys.shape[1]
    lat_width = key_width - ROPE
    seq_count = lax.axis_size("seq")
    seq_len = row_total // CPG
    block_len = seq_len // NBLK
    summ_len = block_len // 2
    total_cands = CPG * seq_count
    group_index = lax.axis_index("seq")
    row_ids = jnp.arange(row_total, dtype=jnp.int32)
    row_local = row_ids // seq_len
    row_pos = row_ids % seq_len
    row_table = (group_index * CPG + row_local) * NBLK + row_pos // block_len
    table_pick = (
        row_table[:, None] == jnp.arange(total_cands * NBLK, dtype=jnp.int32)[None, :]
    ).astype(jnp.float32)
    mask_rows = jnp.dot(
        table_pick,
        block_mask.reshape(total_cands * NBLK, NBLK + total_cands).astype(jnp.float32),
        preferred_element_type=jnp.float32,
    )
    gathered = lax.all_gather(keys, "exp", axis=0, tiled=True)
    pieces = []
    for member in range(CPG):
        first_pos = jnp.take(summary_start, group_index * CPG + member)
        first_row = member * seq_len + first_pos
        pieces.append(lax.dynamic_slice_in_dim(gathered, first_row, summ_len, 0))
    own_slots = jnp.stack(pieces, axis=0)
    summaries = lax.all_gather(own_slots, "seq", axis=0, tiled=True)
    summary_keys = summaries.reshape(total_cands * summ_len, key_width)
    summary_cand = jnp.arange(total_cands * summ_len, dtype=jnp.int32) // summ_len
    summary_pick = (
        jnp.arange(NBLK + total_cands, dtype=jnp.int32)[:, None] == (NBLK + summary_cand)[None, :]
    ).astype(jnp.float32)
    summary_ok = jnp.dot(mask_rows, summary_pick, preferred_element_type=jnp.float32) > 0.5
    key_pos = jnp.arange(seq_len, dtype=jnp.int32)
    key_blocks = (
        jnp.arange(NBLK, dtype=jnp.int32)[:, None] == (key_pos // block_len)[None, :]
    ).astype(jnp.float32)
    block_ok = jnp.dot(mask_rows[:, :NBLK], key_blocks, preferred_element_type=jnp.float32) > 0.5
    causal_ok = block_ok & (key_pos[None, :] <= row_pos[:, None])
    carried = start_state(row_total, head_count, lat_width)
    for member in range(CPG):
        lower = member * seq_len
        allowed = causal_ok & (row_local[:, None] == member)
        carried = absorb_keys(
            carried, queries, gathered[lower : lower + seq_len], allowed, lat_width
        )
    carried = absorb_keys(carried, queries, summary_keys, summary_ok, lat_width)
    return (carried[2] / carried[1][..., None]).astype(jnp.bfloat16)


def solution(mesh):
    placed = (P("seq", "exp", None), P(("seq", "exp"), None), P(), P())
    return jax.shard_map(
        shards, mesh=mesh, in_specs=placed, out_specs=P("seq", "exp", None), check_vma=False
    )
```

profile of v0, /device:TPU:0, one launch (start us, length us, event | category | flops | bytes accessed | tf_op | source)
XLA Modules:
  0.0 109.9 jit_solution(4053768190577654757)
XLA Ops:
  6.5 0.0 all-gather.2.cloned.1.call-start
  6.5 0.7 all-gather.2.cloned.1.call-update
  7.3 1.3 %fusion.67 = (s32[1]{0:T(128)}, s32[1]{0:T(128)}) fusion(s32[4]{0:T(128)} %param.7, s32[]{:T(128)S(6)} %select_n.109, s32[]{:T(128)S(6)} %select_n.112), kind=kLoop, calls=%fused_computation.107 | loop fusion | bytes 24 | solution.py:69
  9.9 0.7 convert_element_type.21
  10.6 0.3 fusion.32
  10.9 0.4 convolution_compare_fusion
  11.3 0.4 copy.35
  11.8 1.6 %broadcast_and_fusion.1 = (pred[1024,512]{1,0:T(8,128)(4,1)S(1)}, pred[1024,512]{1,0:T(8,128)(4,1)S(1)}) fusion(pred[1024]{0:T(1024)(128)(4,1)S(1)} %get-tuple-element.47, pred[1024]{0:T(1024)(128)(4,1)S(1)} %get-tuple-element.46, s32[1024]{0:T(1024)S(1)} %fusion.35, s32[512]{0:T(512)S(1)} %add_select_fusion.2, bf16[1024,8]{0,1:T(8,128)(2,1)S(1)} %fusion.32), kind=kOutput, calls=%fused_computation.37 | convolution fusion | flops 6817792 | bytes 1064960 | tf_op jit(solution)/shard_map/dot_general | solution.py:84
  13.3 0.9 copy.29
  14.3 0.9 copy.32
  15.2 35.8 %all-gather.2.cloned.1.call-done = bf16[1024,576]{1,0:T(8,128)(2,1)} async-done(((bf16[64,576]{1,0:T(8,128)(2,1)}), bf16[1024,576]{1,0:T(8,128)(2,1)}) %all-gather.2.cloned.1.call-update) | async-done | bytes 1179664 | tf_op jit(solution)/shard_map/all_gather | solution.py:66
  51.0 1.1 dynamic-slice_bitcast_fusion.1
  52.1 7.2 %all_gather.7 = bf16[4,64,576]{2,1,0:T(8,128)(2,1)S(1)} all-gather(bf16[2,64,576]{2,1,0:T(8,128)(2,1)S(1)} %pad_maximum_fusion), channel_id=1, replica_groups=mesh['seq'=2,'exp'=16] {'seq'}, dimensions={0}, use_global_device_ids=true | all-gather | bytes 442368 | tf_op jit(solution)/shard_map/all_gather | solution.py:73
  59.3 4.6 %fusion.20 = (f32[1024,4]{0,1:T(4,128)S(1)}, f32[256,1024,4]{1,0,2:T(8,128)S(1)}) fusion(pred[1024,256]{0,1:T(8,128)(4,1)S(1)} %copy.35, bf16[256,576,1]{1,0,2:T(8,128)(2,1)S(1)} %bitcast.51, bf16[1024,4,576]{0,2,1:T(8,128)(2,1)} %param.4), kind=kOutput, calls=%fused_computation.25 | convolution fusion | flops 1211101184 | bytes 9486336 | tf_op jit(solution)/shard_map/rhd,kd->rhk/dot_general | solution.py:18
  63.9 0.0 slice-start.1
  63.9 5.8 %fusion.1 = (f32[1024,4]{0,1:T(4,128)S(1)}, f32[1024,4,512]{0,2,1:T(8,128)S(1)}) fusion(pred[1024,512]{0,1:T(8,128)(4,1)S(1)} %copy.32, bf16[1024,4,576]{0,2,1:T(8,128)(2,1)} %param.4, bf16[1024,576]{1,0:T(8,128)(2,1)S(1)} %copy-done), kind=kOutput, calls=%fused_computation.6 | convolution fusion | flops 2422206464 | bytes 14303232 | tf_op jit(solution)/shard_map/rhd,kd->rhk/dot_general | solution.py:18
  69.8 4.1 %fusion = (f32[1024,4]{0,1:T(4,128)S(1)}, f32[1024,4,512]{0,2,1:T(8,128)S(1)}) fusion(pred[1024,512]{0,1:T(8,128)(4,1)S(1)} %copy.29, bf16[1024,4,576]{0,2,1:T(8,128)(2,1)S(1)} %bitcast.55, bf16[1024,576]{1,0:T(8,128)(2,1)S(1)} %copy-done), kind=kOutput, calls=%fused_computation.5 | convolution fusion | flops 2422206464 | bytes 14303232 | tf_op jit(solution)/shard_map/rhd,kd->rhk/dot_general | solution.py:18
  73.8 2.1 %fusion.2 = f32[1024,4]{0,1:T(4,128)S(1)} fusion(f32[1024,4,512]{0,2,1:T(8,128)S(1)} %get-tuple-element.45, f32[1024,4]{0,1:T(4,128)S(1)} %get-tuple-element.37, pred[1024,512]{0,1:T(8,128)(4,1)S(1)} %copy.29), kind=kLoop, calls=%fused_computation.7 | loop fusion | flops 10481664 | bytes 8945664 | tf_op jit(solution)/shard_map/reduce_sum | solution.py:25
  76.0 1.1 fusion.21
  77.0 2.3 %fusion.4 = f32[1024,4]{0,1:T(4,128)S(1)} fusion(f32[1024,4,512]{0,2,1:T(8,128)S(1)} %get-tuple-element.43, f32[1024,4]{0,1:T(4,128)S(1)} %get-tuple-element.31, pred[1024,512]{0,1:T(8,128)(4,1)S(1)} %copy.32), kind=kLoop, calls=%fused_computation.9 | loop fusion | flops 10481664 | bytes 8945664 | tf_op jit(solution)/shard_map/reduce_sum | solution.py:25
  79.4 6.1 %fusion.8 = f32[1024,4,512]{2,0,1:T(8,128)} fusion(f32[1024,4,512]{0,2,1:T(8,128)S(1)} %get-tuple-element.45, f32[1024,4]{0,1:T(4,128)S(1)} %get-tuple-element.37, pred[1024,512]{0,1:T(8,128)(4,1)S(1)} %copy.29, bf16[1024,576]{1,0:T(8,128)(2,1)S(1)} %copy-done), kind=kOutput, calls=%fused_computation.12 | convolution fusion | flops 2157969408 | bytes 17842176 | tf_op jit(solution)/shard_map/rhk,kd->rhd/dot_general | solution.py:26
  85.5 6.1 %fusion.6 = f32[1024,4,512]{2,0,1:T(8,128)} fusion(f32[1024,4,512]{0,2,1:T(8,128)S(1)} %get-tuple-element.43, f32[1024,4]{0,1:T(4,128)S(1)} %get-tuple-element.31, pred[1024,512]{0,1:T(8,128)(4,1)S(1)} %copy.32, bf16[1024,576]{1,0:T(8,128)(2,1)S(1)} %copy-done), kind=kOutput, calls=%fused_computation.11 | convolution fusion | flops 2157969408 | bytes 17842176 | tf_op jit(solution)/shard_map/rhk,kd->rhd/dot_general | solution.py:26
  91.6 6.2 %divide_convert_fusion = bf16[1024,4,512]{2,0,1:T(8,128)(2,1)S(1)} fusion(f32[1024,4,512]{2,0,1:T(8,128)} %fusion.6, f32[1024,4,512]{2,0,1:T(8,128)S(1)} %copy-done.1, f32[1024,4]{0,1:T(4,128)S(1)} %get-tuple-element.27, f32[1024,4]{0,1:T(4,128)S(1)} %get-tuple-element.29, f32[1024,4]{0,1:T(4,128)S(1)} %get-tuple-element.28, ...), kind=kOutput, calls=%fused_computation | convolution fusion | flops 1093664768 | bytes 25772032 | tf_op jit(solution)/shard_map/rhk,kd->rhd/dot_general | solution.py:26
  97.8 5.2 %copy.38 = bf16[1024,4,512]{2,1,0:T(4,128)(2,1)} copy(bf16[1024,4,512]{2,0,1:T(8,128)(2,1)S(1)} %divide_convert_fusion) | data formatting | bytes 8388608 | tf_op jit(solution)/shard_map/convert_element_type | solution.py:94
  (16 shorter events, 0.1 us)
Async XLA Ops:
  6.5 44.5 %all-gather.2.cloned.1.call-start = ((), (), s32[]{:S(2)}) async-start(), calls=%async_computation | async-start | bytes 1392640 | tf_op jit(solution)/shard_map/all_gather | solution.py:66
  51.0 12.9 %copy-start = (bf16[1024,576]{1,0:T(8,128)(2,1)S(1)}, bf16[1024,576]{1,0:T(8,128)(2,1)}, u32[]{:S(2)}) copy-start(bf16[1024,576]{1,0:T(8,128)(2,1)} %all-gather.2.cloned.1.call-done) | copy-start | bytes 3538948
  59.3 10.4 %slice-start = ((s8[4718592]{0:T(1024)(128)(4,1)}), s8[4194304]{0:T(1024)(128)(4,1)S(1)}, s32[]{:S(2)}) async-start(s8[4718592]{0:T(1024)(128)(4,1)} %bitcast.54), calls=%async_computation.1 | async-start | bytes 8388608
  63.9 5.8 %slice-start.1 = ((s8[4718592]{0:T(1024)(128)(4,1)}), s8[524288]{0:T(1024)(128)(4,1)S(1)}, s32[]{:S(2)}) async-start(s8[4718592]{0:T(1024)(128)(4,1)} %bitcast.54), calls=%async_computation.2 | async-start | bytes 1048576
  85.5 6.1 %copy-start.1 = (f32[1024,4,512]{2,0,1:T(8,128)S(1)}, f32[1024,4,512]{2,0,1:T(8,128)}, u32[]{:S(2)}) copy-start(f32[1024,4,512]{2,0,1:T(8,128)} %fusion.8) | copy-start | bytes 25165828
Sparse Core Ops, SparseCore 0:
  9.6 41.3 all-gather.1
where the time goes:
time: 110 us
  waiting for transfers between devices  36.5 us (33%)
  matrix products  35.1 us (32%)
  between operations  14.9 us (14%)
  local copies, waits for them, and re-layouts  9.99 us (9%)
  blocking collectives  7.17 us (7%)
  other arithmetic  6.32 us (6%)
    all_gather x1, waiting for transfers between devices, shards(): gathered = lax.all_gather(keys, 'exp', axis=0, tiled=True)  35.8 us
    dot_general x3, matrix products, absorb_keys(): jnp.einsum('rhk,kd->rhd', weights.astype(jnp.bfloat16), block_keys[:, :la...  18.4 us
    dot_general x3, matrix products, absorb_keys(): jnp.einsum('rhd,kd->rhk', query_rows, block_keys, preferred_element_type=...  14.5 us
    all_gather x1, blocking collectives, shards(): summaries = lax.all_gather(own_slots, 'seq', axis=0, tiled=True)  7.17 us
    reduce_sum x3, other arithmetic, absorb_keys(): weight_sum = weight_sum * factor + jnp.sum(weights, axis=2)  5.5 us
    convert_element_type x1, local copies, waits for them, and re-layouts, shards(): return (carried[2] / carried[1][..., None]).astype(jnp.bfloat16)  5.25 us
  transfers between devices with their start and end apart: 1, of which 1 were waited for; matrix products, arithmetic and copies ran while one was open for 6% of the time, Pallas kernels for 0%

commit v1 on v0

v1 whole, which is shorter than its diff:
```python
import functools
import math

import jax
import jax.numpy as jnp
from jax import lax
from jax.experimental import pallas as pl
from jax.experimental.pallas import tpu as pltpu
from jax.sharding import PartitionSpec as P

ROPE = 64
NBLK = 4
TILE = 256

score_scale = 192.0 ** (-0.5) * math.log2(math.e)
neg_big = -1e30


def step_orders(count):
    bits = [1 << k for k in range(1, count.bit_length() - 1)]
    bits.reverse()
    first = bits[:1] + bits[:0:-1]
    return first, first[-1:] + first[:-1]


def slot_offsets(order):
    offsets = [0]
    for bit in order:
        offsets = offsets + [o ^ bit for o in offsets]
    return offsets


def gather_steps(keys):
    count = lax.axis_size("exp")
    first, second = step_orders(count)
    held = keys
    for bit_a, bit_b in zip(first, second):
        pairs = [(i, i ^ (bit_b if i & 1 else bit_a)) for i in range(count)]
        held = jnp.concatenate([held, lax.ppermute(held, "exp", pairs)], axis=0)
    other = lax.ppermute(held, "exp", [(i, i ^ 1) for i in range(count)])
    return held, other


def order_kernel(cpg, offsets_a, offsets_b, start_ref, held_ref, other_ref, keys_ref, own_ref):
    me = lax.axis_index("exp")
    group = lax.axis_index("seq")
    part = me % 2
    shard = held_ref.shape[0] // len(offsets_a)
    for s, (a, b) in enumerate(zip(offsets_a, offsets_b)):
        rows = slice(s * shard, (s + 1) * shard)
        here = (me ^ jnp.where(part == 0, a, b)) * shard
        there = (me ^ 1 ^ jnp.where(part == 0, b, a)) * shard
        keys_ref[pl.ds(pl.multiple_of(here, shard), shard), :] = held_ref[rows, :]
        keys_ref[pl.ds(pl.multiple_of(there, shard), shard), :] = other_ref[rows, :]
    summ = own_ref.shape[0] // cpg
    length = keys_ref.shape[0] // cpg
    for member in range(cpg):
        row = member * length + start_ref[group * cpg + member]
        own_ref[member * summ : (member + 1) * summ, :] = keys_ref[
            pl.ds(pl.multiple_of(row, summ), summ), :
        ]


def attend_kernel(dims, mask_ref, q_ref, keys_ref, sums_ref, out_ref, near, staged, sem):
    heads, cpg, cands, length, block, summ, lat = dims
    width = q_ref.shape[2]
    group = lax.axis_index("seq")
    steps = cpg * NBLK
    near[...] = jnp.zeros_like(near)

    def out_copy(i, slot):
        return pltpu.make_async_copy(
            staged.at[slot], out_ref.at[pl.ds(i * block, block)], sem.at[slot]
        )

    def step(i, _):
        slot = lax.rem(i, 2)
        member, b = i // NBLK, lax.rem(i, NBLK)
        base = ((group * cpg + member) * NBLK + b) * (NBLK + cands)
        near[0:block, :] = keys_ref[pl.ds(pl.multiple_of(i * block, block), block), :]
        n = jnp.int32(block)
        for j in range(NBLK - 1):
            seen = jnp.logical_and(j < b, mask_ref[base + j] == 1)

            @pl.when(seen)
            def _():
                near[pl.ds(pl.multiple_of(n, summ), block), :] = keys_ref[
                    pl.ds(pl.multiple_of(member * length + j * block, block), block), :
                ]

            n = n + jnp.where(seen, block, 0)
        for d in range(cands):
            seen = mask_ref[base + NBLK + d] == 1
            row = ((group ^ (d // cpg)) * cpg + d % cpg) * summ

            @pl.when(seen)
            def _():
                near[pl.ds(pl.multiple_of(n, summ), summ), :] = sums_ref[
                    pl.ds(pl.multiple_of(row, summ), summ), :
                ]

            n = n + jnp.where(seen, summ, 0)
        tiles = (n + TILE - 1) // TILE

        @pl.when(i >= 2)
        def _():
            out_copy(i - 2, slot).wait()

        def attend(tile_total):
            total = TILE * tile_total
            rows = heads * block
            q = q_ref[:, pl.ds(pl.multiple_of(i * block, block), block), :].reshape(rows, width)
            scores = lax.dot_general(
                q, near[:total, :], (((1,), (1,)), ((), ())), preferred_element_type=jnp.float32
            )
            pos = lax.rem(lax.broadcasted_iota(jnp.int32, (rows, 1), 0), block)
            col = lax.broadcasted_iota(jnp.int32, (1, total), 1)
            least = jnp.where(col < block, col, jnp.where(col < n, -1, block))
            scores = jnp.where(least <= pos, scores * score_scale, neg_big)
            weights = jnp.exp2(scores - jnp.max(scores, axis=1, keepdims=True))
            weight_sum = jnp.sum(weights, axis=1, keepdims=True)
            numerator = lax.dot_general(
                weights.astype(jnp.bfloat16),
                near[:total, :lat],
                (((1,), (0,)), ((), ())),
                preferred_element_type=jnp.float32,
            )
            result = (numerator * (1.0 / weight_sum)).astype(jnp.bfloat16)
            staged[slot] = jnp.swapaxes(result.reshape(heads, block, lat), 0, 1)

        for tile_total in range(1, near.shape[0] // TILE + 1):
            pl.when(tiles == tile_total)(functools.partial(attend, tile_total))
        out_copy(i, slot).start()
        return 0

    lax.fori_loop(0, steps, step, 0)
    for i in range(max(steps - 2, 0), steps):
        out_copy(i, i % 2).wait()


def shards(queries, keys, block_mask, summary_start):
    row_total, head_count, key_width = queries.shape
    lat_width = key_width - ROPE
    seq_count = lax.axis_size("seq")
    total_cands = block_mask.shape[0]
    cpg = total_cands // seq_count
    seq_len = row_total // cpg
    block_len = seq_len // NBLK
    summ_len = block_len // 2
    most = NBLK * block_len + (total_cands - 1) * summ_len
    most = -(-most // TILE) * TILE
    vmem = pl.BlockSpec(memory_space=pltpu.VMEM)
    smem = pl.BlockSpec(memory_space=pltpu.SMEM)

    by_head = jnp.transpose(queries, (1, 0, 2))
    held, other = gather_steps(keys)
    first, second = step_orders(lax.axis_size("exp"))
    ordered, own = pl.pallas_call(
        functools.partial(order_kernel, cpg, slot_offsets(first), slot_offsets(second)),
        out_shape=[
            jax.ShapeDtypeStruct((row_total, key_width), keys.dtype),
            jax.ShapeDtypeStruct((cpg * summ_len, key_width), keys.dtype),
        ],
        in_specs=[smem, vmem, vmem],
        out_specs=[vmem, vmem],
        name="order",
    )(summary_start, held, other)
    sums = own
    bit = 1
    while bit < seq_count:
        pairs = [(i, i ^ bit) for i in range(seq_count)]
        sums = jnp.concatenate([sums, lax.ppermute(sums, "seq", pairs)], axis=0)
        bit *= 2
    dims = (head_count, cpg, total_cands, seq_len, block_len, summ_len, lat_width)
    return pl.pallas_call(
        functools.partial(attend_kernel, dims),
        out_shape=jax.ShapeDtypeStruct((row_total, head_count, lat_width), queries.dtype),
        in_specs=[smem, vmem, vmem, vmem],
        out_specs=pl.BlockSpec(memory_space=pl.ANY),
        scratch_shapes=[
            pltpu.VMEM((most, key_width), keys.dtype),
            pltpu.VMEM((2, block_len, head_count, lat_width), queries.dtype),
            pltpu.SemaphoreType.DMA((2,)),
        ],
        compiler_params=pltpu.CompilerParams(vmem_limit_bytes=24 << 20),
        name="attend",
    )(block_mask.reshape(-1), by_head, ordered, sums)


def solution(mesh):
    placed = (P("seq", "exp", None), P(("seq", "exp"), None), P(), P())
    return jax.shard_map(
        shards, mesh=mesh, in_specs=placed, out_specs=P("seq", "exp", None), check_vma=False
    )
```

time: 110 us -> 50.7 us (0.46)
  matrix products: 35.1 us -> 0 us
  waiting for transfers between devices: 36.5 us -> 12.2 us
  between operations: 14.9 us -> 0.09 us
  Pallas kernels: 0 us -> 13.5 us
  starting transfers between devices: 0.01 us -> 9.93 us
  blocking collectives: 7.17 us -> 0 us
  other arithmetic: 6.32 us -> 1.85 us
  local copies, waits for them, and re-layouts: 9.99 us -> 12.7 us
    all_gather x1 -> x0, waiting for transfers between devices: 35.8 us -> none  [shards(): gathered = lax.all_gather(keys, 'exp', axis=0, tiled=True)]
    dot_general x9 -> x0, matrix products: 35.1 us -> none  [the longest x3 18.4 us: absorb_keys(): jnp.einsum('rhk,kd->rhd', weights.astype(jnp.bfloat16), block_keys[:, :la...]
    pallas_call x0 -> x2, Pallas kernels: none -> 13.5 us  [the longest x1 11 us: shards(): pl.pallas_call(functools.partial(attend_kernel, dims), out_shape=jax.Shap...]
    ppermute x0 -> x5, waiting for transfers between devices: none -> 12.2 us  [the longest x3 10.2 us: gather_steps(): held = jnp.concatenate([held, lax.ppermute(held, 'exp', pairs)], axis=0)]
    unnamed x8 -> x14, local copies, waits for them, and re-layouts: 0.02 us -> 11.2 us
    ppermute x0 -> x5, starting transfers between devices: none -> 9.93 us  [the longest x3 8.04 us: gather_steps(): held = jnp.concatenate([held, lax.ppermute(held, 'exp', pairs)], axis=0)]
    all_gather x1 -> x0, blocking collectives: 7.17 us -> none  [shards(): summaries = lax.all_gather(own_slots, 'seq', axis=0, tiled=True)]
    reduce_sum x3 -> x0, other arithmetic: 5.5 us -> none  [absorb_keys(): weight_sum = weight_sum * factor + jnp.sum(weights, axis=2)]
  transfers between devices with their start and end apart: 1 -> 5, of which waited for: 1 -> 4; matrix products, arithmetic and copies ran while one was open for 6% -> 18% of each run, Pallas kernels for 0% -> 0%
where the time goes in v1:
time: 50.7 us; the launch traced here: 50.3 us
  Pallas kernels  13.5 us (27%)
  local copies, waits for them, and re-layouts  12.7 us (25%)
  waiting for transfers between devices  12.2 us (24%)
  starting transfers between devices  9.93 us (20%)
  other arithmetic  1.85 us (4%)
    unnamed x14, local copies, waits for them, and re-layouts  11.2 us
    pallas_call x1, Pallas kernels, shards(): pl.pallas_call(functools.partial(attend_kernel, dims), out_shape=jax.Shap...  11 us
    ppermute x3, waiting for transfers between devices, gather_steps(): held = jnp.concatenate([held, lax.ppermute(held, 'exp', pairs)], axis=0)  10.2 us
    ppermute x3, starting transfers between devices, gather_steps(): held = jnp.concatenate([held, lax.ppermute(held, 'exp', pairs)], axis=0)  8.04 us
    pallas_call x1, Pallas kernels, shards(): pl.pallas_call(functools.partial(order_kernel, cpg, slot_offsets(first),...  2.5 us
    ppermute x1, waiting for transfers between devices, gather_steps(): other = lax.ppermute(held, 'exp', [(i, i ^ 1) for i in range(count)])  1.99 us
    ppermute x1, starting transfers between devices, shards(): sums = jnp.concatenate([sums, lax.ppermute(sums, 'seq', pairs)], axis=0)  1.82 us
    concatenate x2, other arithmetic, gather_steps(): held = jnp.concatenate([held, lax.ppermute(held, 'exp', pairs)], axis=0)  1.82 us
  transfers between devices with their start and end apart: 5, of which 4 were waited for; matrix products, arithmetic and copies ran while one was open for 18% of the time, Pallas kernels for 0%

profile of v1, /device:TPU:0, one launch (start us, length us, event | category | flops | bytes accessed | tf_op | source)
XLA Modules:
  0.0 50.3 jit_solution(2106291851972341784)
XLA Ops:
  0.0 4.1 %collective-permute-start = (bf16[64,576]{1,0:T(8,128)(2,1)}, bf16[64,576]{1,0:T(8,128)(2,1)S(1)}, u32[]{:S(2)}, u32[]{:S(2)}) collective-permute-start(bf16[64,576]{1,0:T(8,128)(2,1)} %param.5), channel_id=1, source_target_pairs={{0,8},{1,5},{2,10},{3,7},{4,12},{5,1},{6,14},{7,3},{8,0},{9,13},{1... | collective-permute-start | bytes 221192 | tf_op jit(solution)/shard_map/ppermute | solution.py:39
  4.1 2.6 %collective-permute-done = bf16[64,576]{1,0:T(8,128)(2,1)S(1)} collective-permute-done((bf16[64,576]{1,0:T(8,128)(2,1)}, bf16[64,576]{1,0:T(8,128)(2,1)S(1)}, u32[]{:S(2)}, u32[]{:S(2)}) %collective-permute-start) | collective-permute-done | bytes 73760 | tf_op jit(solution)/shard_map/ppermute | solution.py:39
  6.7 0.9 %pad_maximum_fusion.2 = bf16[128,576]{1,0:T(8,128)(2,1)S(1)} fusion(bf16[64,576]{1,0:T(8,128)(2,1)S(1)} %collective-permute-done, bf16[64,576]{1,0:T(8,128)(2,1)} %param.5), kind=kLoop, calls=%fused_computation.2 | loop fusion | flops 294912 | bytes 294912 | tf_op jit(solution)/shard_map/concatenate | solution.py:39
  7.6 1.9 %collective-permute-start.1 = (bf16[128,576]{1,0:T(8,128)(2,1)S(1)}, bf16[128,576]{1,0:T(8,128)(2,1)S(1)}, u32[]{:S(2)}, u32[]{:S(2)}) collective-permute-start(bf16[128,576]{1,0:T(8,128)(2,1)S(1)} %pad_maximum_fusion.2), channel_id=1, source_target_pairs={{0,2},{1,9},{2,0},{3,11},{4,6},{5,13},{6,4},{7,15},{8,10},{9,1},{1... | collective-permute-start | bytes 442376 | tf_op jit(solution)/shard_map/ppermute | solution.py:39
  9.5 3.5 %collective-permute-done.1 = bf16[128,576]{1,0:T(8,128)(2,1)S(1)} collective-permute-done((bf16[128,576]{1,0:T(8,128)(2,1)S(1)}, bf16[128,576]{1,0:T(8,128)(2,1)S(1)}, u32[]{:S(2)}, u32[]{:S(2)}) %collective-permute-start.1) | collective-permute-done | bytes 147488 | tf_op jit(solution)/shard_map/ppermute | solution.py:39
  13.0 0.9 %pad_maximum_fusion = bf16[256,576]{1,0:T(8,128)(2,1)S(1)} fusion(bf16[128,576]{1,0:T(8,128)(2,1)S(1)} %collective-permute-done.1, bf16[64,576]{1,0:T(8,128)(2,1)S(1)} %collective-permute-done, bf16[64,576]{1,0:T(8,128)(2,1)} %param.5), kind=kLoop, calls=%fused_computation | loop fusion | flops 884736 | bytes 589824 | tf_op jit(solution)/shard_map/concatenate | solution.py:39
  13.9 2.1 %collective-permute-start.2 = (bf16[256,576]{1,0:T(8,128)(2,1)S(1)}, bf16[256,576]{1,0:T(8,128)(2,1)S(1)}, u32[]{:S(2)}, u32[]{:S(2)}) collective-permute-start(bf16[256,576]{1,0:T(8,128)(2,1)S(1)} %pad_maximum_fusion), channel_id=1, source_target_pairs={{0,4},{1,3},{2,6},{3,1},{4,0},{5,7},{6,2},{7,5},{8,12},{9,11},{10,... | collective-permute-start | bytes 884744 | tf_op jit(solution)/shard_map/ppermute | solution.py:39
  16.0 0.9 %constant_dynamic-update-slice_fusion.3 = bf16[512,576]{1,0:T(8,128)(2,1)S(1)} fusion(bf16[64,576]{1,0:T(8,128)(2,1)} %param.5), kind=kLoop, calls=%fused_computation.6 | loop fusion | bytes 155648
  16.9 4.1 %collective-permute-done.2 = bf16[256,576]{1,0:T(8,128)(2,1)S(1)} collective-permute-done((bf16[256,576]{1,0:T(8,128)(2,1)S(1)}, bf16[256,576]{1,0:T(8,128)(2,1)S(1)}, u32[]{:S(2)}, u32[]{:S(2)}) %collective-permute-start.2) | collective-permute-done | bytes 294944 | tf_op jit(solution)/shard_map/ppermute | solution.py:39
  21.1 0.0 copy-start.2
  21.1 0.2 copy.7
  21.3 0.1 collective-permute-start.3
  21.4 2.0 %collective-permute-done.3 = bf16[512,576]{0,1:T(8,128)(2,1)S(1)} collective-permute-done((bf16[512,576]{0,1:T(8,128)(2,1)S(1)}, bf16[512,576]{0,1:T(8,128)(2,1)S(1)}, u32[]{:S(2)}, u32[]{:S(2)}) %collective-permute-start.3) | collective-permute-done | bytes 589856 | tf_op jit(solution)/shard_map/ppermute | solution.py:40
  23.4 1.1 %copy.8.other_ref = bf16[512,576]{1,0:T(8,128)(2,1)} copy(bf16[512,576]{0,1:T(8,128)(2,1)S(1)} %collective-permute-done.3) | data formatting | bytes 1179648 | tf_op jit(solution)/shard_map/ppermute | solution.py:40
  24.5 2.5 %order.1 = (bf16[1024,576]{1,0:T(8,128)(2,1)}, bf16[128,576]{1,0:T(8,128)(2,1)}) custom-call(s32[4]{0:T(128)} %start_ref.1, bf16[512,576]{1,0:T(8,128)(2,1)} %copy-done.2, bf16[512,576]{1,0:T(8,128)(2,1)} %copy.8.other_ref), custom_call_target="tpu_custom_call" | custom-call | tf_op jit(solution)/shard_map/order/pallas_call | solution.py:158
  27.0 1.8 %collective-permute-start.4 = (bf16[128,576]{1,0:T(8,128)(2,1)}, bf16[128,576]{1,0:T(8,128)(2,1)S(1)}, u32[]{:S(2)}, u32[]{:S(2)}) collective-permute-start(bf16[128,576]{1,0:T(8,128)(2,1)} %get-tuple-element.8), channel_id=1, source_target_pairs={{0,16},{16,0},{1,17},{17,1},{2,18},{18,2},{3,19},{19,3},{4,20},{20... | collective-permute-start | bytes 442376 | tf_op jit(solution)/shard_map/ppermute | solution.py:172
  28.8 0.0 copy-done.4
  28.8 0.1 reshape.3.mask_ref
  28.9 0.0 copy-start.3
  29.0 0.0 copy-start.1
  29.0 7.8 %copy.6 = bf16[1024,4,576]{2,0,1:T(8,128)(2,1)} copy(bf16[1024,4,576]{0,2,1:T(8,128)(2,1)} %param.4) | data formatting | bytes 9437184 | tf_op args[0]
  36.8 0.0 collective-permute-done.4
  36.8 2.5 %copy-done = bf16[1024,4,576]{2,0,1:T(8,128)(2,1)S(1)} copy-done((bf16[1024,4,576]{2,0,1:T(8,128)(2,1)S(1)}, bf16[1024,4,576]{2,0,1:T(8,128)(2,1)}, u32[]{:S(2)}) %copy-start) | copy-done | bytes 4718616
  39.3 11.0 %attend.1 = bf16[1024,4,512]{2,1,0:T(4,128)(2,1)} custom-call(s32[128]{0:T(128)S(1)} %reshape.3.mask_ref, bf16[4,1024,576]{2,1,0:T(8,128)(2,1)S(1)} %bitcast.1, bf16[1024,576]{1,0:T(8,128)(2,1)S(1)} %copy-done.1, bf16[256,576]{1,0:T(8,128)(2,1)S(1)} %pad_maximum_fusion.1.sums_ref), custom_call_target="tpu_custom_call" | custom-call | tf_op jit(solution)/shard_map/attend/pallas_call | solution.py:175
  (9 shorter events, 0.1 us)
Async XLA Ops:
  0.0 28.8 %copy-start.4 = (s32[4,4,8]{2,1,0:T(4,128)S(1)}, s32[4,4,8]{2,1,0:T(4,128)}, u32[]{:S(2)}) copy-start(s32[4,4,8]{2,1,0:T(4,128)} %param.6) | copy-start | bytes 1540
  0.0 6.7 %collective-permute-start = (bf16[64,576]{1,0:T(8,128)(2,1)}, bf16[64,576]{1,0:T(8,128)(2,1)S(1)}, u32[]{:S(2)}, u32[]{:S(2)}) collective-permute-start(bf16[64,576]{1,0:T(8,128)(2,1)} %param.5), channel_id=1, source_target_pairs={{0,8},{1,5},{2,10},{3,7},{4,12},{5,1},{6,14},{7,3},{8,0},{9,13},{1... | collective-permute-start | bytes 221192 | tf_op jit(solution)/shard_map/ppermute | solution.py:39
  7.6 5.4 %collective-permute-start.1 = (bf16[128,576]{1,0:T(8,128)(2,1)S(1)}, bf16[128,576]{1,0:T(8,128)(2,1)S(1)}, u32[]{:S(2)}, u32[]{:S(2)}) collective-permute-start(bf16[128,576]{1,0:T(8,128)(2,1)S(1)} %pad_maximum_fusion.2), channel_id=1, source_target_pairs={{0,2},{1,9},{2,0},{3,11},{4,6},{5,13},{6,4},{7,15},{8,10},{9,1},{1... | collective-permute-start | bytes 442376 | tf_op jit(solution)/shard_map/ppermute | solution.py:39
  13.9 7.1 %collective-permute-start.2 = (bf16[256,576]{1,0:T(8,128)(2,1)S(1)}, bf16[256,576]{1,0:T(8,128)(2,1)S(1)}, u32[]{:S(2)}, u32[]{:S(2)}) collective-permute-start(bf16[256,576]{1,0:T(8,128)(2,1)S(1)} %pad_maximum_fusion), channel_id=1, source_target_pairs={{0,4},{1,3},{2,6},{3,1},{4,0},{5,7},{6,2},{7,5},{8,12},{9,11},{10,... | collective-permute-start | bytes 884744 | tf_op jit(solution)/shard_map/ppermute | solution.py:39
  21.1 3.4 %copy-start.2 = (bf16[512,576]{1,0:T(8,128)(2,1)}, bf16[512,576]{1,0:T(8,128)(2,1)S(1)}, u32[]{:S(2)}) copy-start(bf16[512,576]{1,0:T(8,128)(2,1)S(1)} %constant_dynamic-update-slice_fusion.held_ref) | copy-start | bytes 1769476
  21.3 2.1 %collective-permute-start.3 = (bf16[512,576]{0,1:T(8,128)(2,1)S(1)}, bf16[512,576]{0,1:T(8,128)(2,1)S(1)}, u32[]{:S(2)}, u32[]{:S(2)}) collective-permute-start(bf16[512,576]{0,1:T(8,128)(2,1)S(1)} %copy.7), channel_id=1, source_target_pairs={{0,1},{1,0},{2,3},{3,2},{4,5},{5,4},{6,7},{7,6},{8,9},{9,8},{10,11... | collective-permute-start | bytes 1769480 | tf_op jit(solution)/shard_map/ppermute | solution.py:40
  27.0 9.7 %collective-permute-start.4 = (bf16[128,576]{1,0:T(8,128)(2,1)}, bf16[128,576]{1,0:T(8,128)(2,1)S(1)}, u32[]{:S(2)}, u32[]{:S(2)}) collective-permute-start(bf16[128,576]{1,0:T(8,128)(2,1)} %get-tuple-element.8), channel_id=1, source_target_pairs={{0,16},{16,0},{1,17},{17,1},{2,18},{18,2},{3,19},{19,3},{4,20},{20... | collective-permute-start | bytes 442376 | tf_op jit(solution)/shard_map/ppermute | solution.py:172
  28.9 7.8 %copy-start.3 = (bf16[128,576]{1,0:T(8,128)(2,1)S(1)}, bf16[128,576]{1,0:T(8,128)(2,1)}, u32[]{:S(2)}) copy-start(bf16[128,576]{1,0:T(8,128)(2,1)} %get-tuple-element.8) | copy-start | bytes 442372
  29.0 7.8 %copy-start.1 = (bf16[1024,576]{1,0:T(8,128)(2,1)S(1)}, bf16[1024,576]{1,0:T(8,128)(2,1)}, u32[]{:S(2)}) copy-start(bf16[1024,576]{1,0:T(8,128)(2,1)} %get-tuple-element.7.keys_ref) | copy-start | bytes 3538948
  36.8 2.5 %copy-start = (bf16[1024,4,576]{2,0,1:T(8,128)(2,1)S(1)}, bf16[1024,4,576]{2,0,1:T(8,128)(2,1)}, u32[]{:S(2)}) copy-start(bf16[1024,4,576]{2,0,1:T(8,128)(2,1)} %copy.6) | copy-start | bytes 14155780

commit v2 on v1

--- a/solution.py
+++ b/solution.py
@@ -30,28 +30,80 @@
     return offsets
 
 
-def gather_steps(keys):
+def grant(mib):
+    return pltpu.CompilerParams(vmem_limit_bytes=mib << 20)
+
+
+def join_kernel(first_ref, second_ref, out_ref):
+    half = first_ref.shape[0]
+    out_ref[:half] = first_ref[...]
+    out_ref[half:] = second_ref[...]
+
+
+def join(first, second):
+    vmem = pl.BlockSpec(memory_space=pltpu.VMEM)
+    return pl.pallas_call(
+        join_kernel,
+        out_shape=jax.ShapeDtypeStruct((2 * first.shape[0],) + first.shape[1:], first.dtype),
+        in_specs=[vmem, vmem],
+        out_specs=vmem,
+        compiler_params=grant(2),
+        name="join",
+    )(first, second)
+
+
+def turn_kernel(in_ref, out_ref):
+    for h in range(in_ref.shape[0]):
+        out_ref[h] = in_ref[h].T
+
+
+def turn(by_width, head, total):
+    _, width, rows = by_width.shape
+    cut = min(rows, 256)
+    return pl.pallas_call(
+        turn_kernel,
+        out_shape=jax.ShapeDtypeStruct((total, rows, width), by_width.dtype),
+        grid=(total, rows // cut),
+        in_specs=[pl.BlockSpec((1, width, cut), lambda h, i: (head + h, 0, i))],
+        out_specs=pl.BlockSpec((1, cut, width), lambda h, i: (h, i, 0)),
+        compiler_params=grant(4),
+        name="turn",
+    )(by_width)
+
+
+def gather_steps(keys, queries):
     count = lax.axis_size("exp")
+    heads = queries.shape[1]
     first, second = step_orders(count)
-    held = keys
-    for bit_a, bit_b in zip(first, second):
+    last = len(first)
+    by_width = jnp.transpose(queries, (1, 2, 0))
+    by_head = []
+    done = 0
+    held = keys[None]
+    for k, (bit_a, bit_b) in enumerate(zip(first, second)):
         pairs = [(i, i ^ (bit_b if i & 1 else bit_a)) for i in range(count)]
-        held = jnp.concatenate([held, lax.ppermute(held, "exp", pairs)], axis=0)
+        got = lax.ppermute(held, "exp", pairs)
+        due = heads if k == last - 1 else heads * (k + 1) // (last + 1)
+        if due > done:
+            piece = turn(by_width, done, due - done)
+            got, piece = lax.optimization_barrier((got, piece))
+            by_head.append(piece)
+            done = due
+        held = join(held, got)
     other = lax.ppermute(held, "exp", [(i, i ^ 1) for i in range(count)])
-    return held, other
+    return held, other, by_head
 
 
 def order_kernel(cpg, offsets_a, offsets_b, start_ref, held_ref, other_ref, keys_ref, own_ref):
     me = lax.axis_index("exp")
     group = lax.axis_index("seq")
     part = me % 2
-    shard = held_ref.shape[0] // len(offsets_a)
+    shard = held_ref.shape[1]
     for s, (a, b) in enumerate(zip(offsets_a, offsets_b)):
-        rows = slice(s * shard, (s + 1) * shard)
         here = (me ^ jnp.where(part == 0, a, b)) * shard
         there = (me ^ 1 ^ jnp.where(part == 0, b, a)) * shard
-        keys_ref[pl.ds(pl.multiple_of(here, shard), shard), :] = held_ref[rows, :]
-        keys_ref[pl.ds(pl.multiple_of(there, shard), shard), :] = other_ref[rows, :]
+        keys_ref[pl.ds(pl.multiple_of(here, shard), shard), :] = held_ref[s]
+        keys_ref[pl.ds(pl.multiple_of(there, shard), shard), :] = other_ref[s]
     summ = own_ref.shape[0] // cpg
     length = keys_ref.shape[0] // cpg
     for member in range(cpg):
@@ -61,9 +113,9 @@
         ]
 
 
-def attend_kernel(dims, mask_ref, q_ref, keys_ref, sums_ref, out_ref, near, staged, sem):
+def attend_kernel(dims, mask_ref, keys_ref, sums_ref, *refs):
     heads, cpg, cands, length, block, summ, lat = dims
-    width = q_ref.shape[2]
+    q_refs, (out_ref, near, staged, sem) = refs[:-4], refs[-4:]
     group = lax.axis_index("seq")
     steps = cpg * NBLK
     near[...] = jnp.zeros_like(near)
@@ -76,11 +128,11 @@
     def step(i, _):
         slot = lax.rem(i, 2)
         member, b = i // NBLK, lax.rem(i, NBLK)
-        base = ((group * cpg + member) * NBLK + b) * (NBLK + cands)
+        cand = group * cpg + member
         near[0:block, :] = keys_ref[pl.ds(pl.multiple_of(i * block, block), block), :]
         n = jnp.int32(block)
         for j in range(NBLK - 1):
-            seen = jnp.logical_and(j < b, mask_ref[base + j] == 1)
+            seen = jnp.logical_and(j < b, mask_ref[cand, b, j] == 1)
 
             @pl.when(seen)
             def _():
@@ -90,7 +142,7 @@
 
             n = n + jnp.where(seen, block, 0)
         for d in range(cands):
-            seen = mask_ref[base + NBLK + d] == 1
+            seen = mask_ref[cand, b, NBLK + d] == 1
             row = ((group ^ (d // cpg)) * cpg + d % cpg) * summ
 
             @pl.when(seen)
@@ -109,7 +161,10 @@
         def attend(tile_total):
             total = TILE * tile_total
             rows = heads * block
-            q = q_ref[:, pl.ds(pl.multiple_of(i * block, block), block), :].reshape(rows, width)
+            at = pl.ds(pl.multiple_of(i * block, block), block)
+            q = jnp.concatenate(
+                [q_ref[h, at, :] for q_ref in q_refs for h in range(q_ref.shape[0])], axis=0
+            )
             scores = lax.dot_general(
                 q, near[:total, :], (((1,), (1,)), ((), ())), preferred_element_type=jnp.float32
             )
@@ -152,8 +207,7 @@
     vmem = pl.BlockSpec(memory_space=pltpu.VMEM)
     smem = pl.BlockSpec(memory_space=pltpu.SMEM)
 
-    by_head = jnp.transpose(queries, (1, 0, 2))
-    held, other = gather_steps(keys)
+    held, other, by_head = gather_steps(keys, queries)
     first, second = step_orders(lax.axis_size("exp"))
     ordered, own = pl.pallas_call(
         functools.partial(order_kernel, cpg, slot_offsets(first), slot_offsets(second)),
@@ -163,28 +217,29 @@
         ],
         in_specs=[smem, vmem, vmem],
         out_specs=[vmem, vmem],
+        compiler_params=grant(4),
         name="order",
     )(summary_start, held, other)
     sums = own
     bit = 1
     while bit < seq_count:
         pairs = [(i, i ^ bit) for i in range(seq_count)]
-        sums = jnp.concatenate([sums, lax.ppermute(sums, "seq", pairs)], axis=0)
+        sums = join(sums, lax.ppermute(sums, "seq", pairs))
         bit *= 2
     dims = (head_count, cpg, total_cands, seq_len, block_len, summ_len, lat_width)
     return pl.pallas_call(
         functools.partial(attend_kernel, dims),
         out_shape=jax.ShapeDtypeStruct((row_total, head_count, lat_width), queries.dtype),
-        in_specs=[smem, vmem, vmem, vmem],
+        in_specs=[smem, vmem, vmem] + [vmem] * len(by_head),
         out_specs=pl.BlockSpec(memory_space=pl.ANY),
         scratch_shapes=[
             pltpu.VMEM((most, key_width), keys.dtype),
             pltpu.VMEM((2, block_len, head_count, lat_width), queries.dtype),
             pltpu.SemaphoreType.DMA((2,)),
         ],
-        compiler_params=pltpu.CompilerParams(vmem_limit_bytes=24 << 20),
+        compiler_params=grant(24),
         name="attend",
-    )(block_mask.reshape(-1), by_head, ordered, sums)
+    )(block_mask, ordered, sums, *by_head)
 
 
 def solution(mesh):

time: 50.7 us -> 40 us (0.79)
  local copies, waits for them, and re-layouts: 12.7 us -> 2.45 us
  other arithmetic: 1.85 us -> 0 us
  waiting for transfers between devices: 12.2 us -> 13.8 us
  Pallas kernels: 13.5 us -> 14.6 us
  starting transfers between devices: 9.93 us -> 8.92 us
    unnamed x14 -> x8, local copies, waits for them, and re-layouts: 11.2 us -> 2.45 us
    pallas_call x0 -> x7, Pallas kernels: none -> 3.22 us  [the longest x3 3.1 us: turn(): pl.pallas_call(turn_kernel, out_shape=jax.ShapeDtypeStruct((total, rows,...]
    concatenate x3 -> x0, other arithmetic: 1.85 us -> none  [the longest x2 1.82 us: gather_steps(): held = jnp.concatenate([held, lax.ppermute(held, 'exp', pairs)], axis=0)]
    pallas_call x1, Pallas kernels: 2.5 us -> 0.67 us  [shards(): pl.pallas_call(functools.partial(order_kernel, cpg, slot_offsets(first),...]
    ppermute x4, waiting for transfers between devices: 10.2 us -> 11.7 us  [the longest x3 6.94 us: gather_steps(): got = lax.ppermute(held, 'exp', pairs)]
    ppermute x1 -> x0, local copies, waits for them, and re-layouts: 1.1 us -> none  [gather_steps(): other = lax.ppermute(held, 'exp', [(i, i ^ 1) for i in range(count)])]
    ppermute x4, starting transfers between devices: 9.86 us -> 8.85 us  [the longest x3 7.29 us: gather_steps(): got = lax.ppermute(held, 'exp', pairs)]
  transfers between devices with their start and end apart: 5 -> 5, of which waited for: 4 -> 4; matrix products, arithmetic and copies ran while one was open for 18% -> 0% of each run, Pallas kernels for 0% -> 8%
where the time goes in v2:
time: 40 us; the launch traced here: 39.9 us
  Pallas kernels  14.6 us (36%)
  waiting for transfers between devices  13.8 us (34%)
  starting transfers between devices  8.92 us (22%)
  local copies, waits for them, and re-layouts  2.45 us (6%)
    pallas_call x1, Pallas kernels, shards(): pl.pallas_call(functools.partial(attend_kernel, dims), out_shape=jax.Shap...  10.8 us
    ppermute x3, starting transfers between devices, gather_steps(): got = lax.ppermute(held, 'exp', pairs)  7.29 us
    ppermute x3, waiting for transfers between devices, gather_steps(): got = lax.ppermute(held, 'exp', pairs)  6.94 us
    ppermute x1, waiting for transfers between devices, shards(): sums = join(sums, lax.ppermute(sums, 'seq', pairs))  4.75 us
    pallas_call x3, Pallas kernels, turn(): pl.pallas_call(turn_kernel, out_shape=jax.ShapeDtypeStruct((total, rows,...  3.1 us
    unnamed x8, local copies, waits for them, and re-layouts  2.45 us
    ppermute x1, waiting for transfers between devices, gather_steps(): other = lax.ppermute(held, 'exp', [(i, i ^ 1) for i in range(count)])  2.08 us
    ppermute x1, starting transfers between devices, shards(): sums = join(sums, lax.ppermute(sums, 'seq', pairs))  1.56 us
  transfers between devices with their start and end apart: 5, of which 4 were waited for; matrix products, arithmetic and copies ran while one was open for 0% of the time, Pallas kernels for 8%

profile of v2, /device:TPU:0, one launch (start us, length us, event | category | flops | bytes accessed | tf_op | source)
XLA Modules:
  0.0 39.9 jit_solution(9846040346450100333)
XLA Ops:
  0.0 4.1 %collective-permute-start = (bf16[1,64,576]{2,1,0:T(8,128)(2,1)}, bf16[1,64,576]{2,1,0:T(8,128)(2,1)S(1)}, u32[]{:S(2)}, u32[]{:S(2)}) collective-permute-start(bf16[1,64,576]{2,1,0:T(8,128)(2,1)} %bitcast.5), channel_id=1, source_target_pairs={{0,8},{1,5},{2,10},{3,7},{4,12},{5,1},{6,14},{7,3},{8,0},{9,13},{1... | collective-permute-start | bytes 221192 | tf_op jit(solution)/shard_map/ppermute | solution.py:85
  4.1 0.0 copy-start
  4.1 2.3 %copy-done = bf16[1024,4,576]{0,2,1:T(8,128)(2,1)S(1)} copy-done((bf16[1024,4,576]{0,2,1:T(8,128)(2,1)S(1)}, bf16[1024,4,576]{0,2,1:T(8,128)(2,1)}, u32[]{:S(2)}) %copy-start) | copy-done | bytes 4718616
  6.4 0.0 copy-start.1
  6.4 0.8 %turn.3.refs_0_ = bf16[1,1024,576]{2,1,0:T(8,128)(2,1)S(1)} custom-call(bf16[4,576,1024]{2,1,0:T(8,128)(2,1)S(1)} %bitcast.2), custom_call_target="tpu_custom_call" | custom-call | tf_op jit(solution)/shard_map/turn/pallas_call | solution.py:63
  7.2 0.0 collective-permute-done.second_ref
  7.2 0.1 copy-done.1
  7.3 1.6 %collective-permute-start.1 = (bf16[2,64,576]{2,1,0:T(8,128)(2,1)S(1)}, bf16[2,64,576]{2,1,0:T(8,128)(2,1)S(1)}, u32[]{:S(2)}, u32[]{:S(2)}) collective-permute-start(bf16[2,64,576]{2,1,0:T(8,128)(2,1)S(1)} %join.4.first_ref), channel_id=1, source_target_pairs={{0,2},{1,9},{2,0},{3,11},{4,6},{5,13},{6,4},{7,15},{8,10},{9,1},{1... | collective-permute-start | bytes 442376 | tf_op jit(solution)/shard_map/ppermute | solution.py:85
  8.9 0.8 %turn.4.refs_1_ = bf16[1,1024,576]{2,1,0:T(8,128)(2,1)S(1)} custom-call(bf16[4,576,1024]{2,1,0:T(8,128)(2,1)S(1)} %bitcast.3), custom_call_target="tpu_custom_call" | custom-call | tf_op jit(solution)/shard_map/turn/pallas_call | solution.py:63
  9.7 3.0 %collective-permute-done.1.second_ref = bf16[2,64,576]{2,1,0:T(8,128)(2,1)S(1)} collective-permute-done((bf16[2,64,576]{2,1,0:T(8,128)(2,1)S(1)}, bf16[2,64,576]{2,1,0:T(8,128)(2,1)S(1)}, u32[]{:S(2)}, u32[]{:S(2)}) %collective-permute-start.1) | collective-permute-done | bytes 147488 | tf_op jit(solution)/shard_map/ppermute | solution.py:85
  12.7 0.0 copy-start.3
  12.7 1.6 %collective-permute-start.2 = (bf16[4,64,576]{2,1,0:T(8,128)(2,1)S(1)}, bf16[4,64,576]{2,1,0:T(8,128)(2,1)S(1)}, u32[]{:S(2)}, u32[]{:S(2)}) collective-permute-start(bf16[4,64,576]{2,1,0:T(8,128)(2,1)S(1)} %join.5.first_ref), channel_id=1, source_target_pairs={{0,4},{1,3},{2,6},{3,1},{4,0},{5,7},{6,2},{7,5},{8,12},{9,11},{10,... | collective-permute-start | bytes 884744 | tf_op jit(solution)/shard_map/ppermute | solution.py:85
  14.4 1.6 %turn.5.refs_2_ = bf16[2,1024,576]{2,1,0:T(8,128)(2,1)S(1)} custom-call(bf16[4,576,1024]{2,1,0:T(8,128)(2,1)S(1)} %bitcast.4), custom_call_target="tpu_custom_call" | custom-call | tf_op jit(solution)/shard_map/turn/pallas_call | solution.py:63
  15.9 0.0 copy-start.2
  16.0 3.9 %collective-permute-done.2.second_ref = bf16[4,64,576]{2,1,0:T(8,128)(2,1)S(1)} collective-permute-done((bf16[4,64,576]{2,1,0:T(8,128)(2,1)S(1)}, bf16[4,64,576]{2,1,0:T(8,128)(2,1)S(1)}, u32[]{:S(2)}, u32[]{:S(2)}) %collective-permute-start.2) | collective-permute-done | bytes 294944 | tf_op jit(solution)/shard_map/ppermute | solution.py:85
  19.9 0.1 join.6.held_ref
  19.9 0.1 collective-permute-start.3
  20.0 2.1 %collective-permute-done.3.other_ref = bf16[8,64,576]{2,1,0:T(8,128)(2,1)S(1)} collective-permute-done((bf16[8,64,576]{2,1,0:T(8,128)(2,1)S(1)}, bf16[8,64,576]{2,1,0:T(8,128)(2,1)S(1)}, u32[]{:S(2)}, u32[]{:S(2)}) %collective-permute-start.3) | collective-permute-done | bytes 589856 | tf_op jit(solution)/shard_map/ppermute | solution.py:93
  22.1 0.0 copy-done.3
  22.1 0.7 %order.1 = (bf16[1024,576]{1,0:T(8,128)(2,1)S(1)}, bf16[128,576]{1,0:T(8,128)(2,1)S(1)}) custom-call(s32[4]{0:T(128)S(1)} %copy-done.3, bf16[8,64,576]{2,1,0:T(8,128)(2,1)S(1)} %join.6.held_ref, bf16[8,64,576]{2,1,0:T(8,128)(2,1)S(1)} %collective-permute-done.3.other_ref), custom_call_target="tpu_custom_call" | custom-call | tf_op jit(solution)/shard_map/order/pallas_call | solution.py:212
  22.8 1.6 %collective-permute-start.4 = (bf16[128,576]{1,0:T(8,128)(2,1)S(1)}, bf16[128,576]{1,0:T(8,128)(2,1)S(1)}, u32[]{:S(2)}, u32[]{:S(2)}) collective-permute-start(bf16[128,576]{1,0:T(8,128)(2,1)S(1)} %get-tuple-element.17.first_ref), channel_id=1, source_target_pairs={{0,16},{16,0},{1,17},{17,1},{2,18},{18,2},{3,19},{19,3},{4,20},{20... | collective-permute-start | bytes 442376 | tf_op jit(solution)/shard_map/ppermute | solution.py:227
  24.3 4.7 %collective-permute-done.4.second_ref = bf16[128,576]{1,0:T(8,128)(2,1)S(1)} collective-permute-done((bf16[128,576]{1,0:T(8,128)(2,1)S(1)}, bf16[128,576]{1,0:T(8,128)(2,1)S(1)}, u32[]{:S(2)}, u32[]{:S(2)}) %collective-permute-start.4) | collective-permute-done | bytes 147488 | tf_op jit(solution)/shard_map/ppermute | solution.py:227
  29.1 0.0 copy-done.2
  29.1 10.8 %attend.1 = bf16[1024,4,512]{2,1,0:T(4,128)(2,1)} custom-call(s32[4,4,8]{2,1,0:T(4,128)S(1)} %copy-done.2, bf16[1024,576]{1,0:T(8,128)(2,1)S(1)} %get-tuple-element.16.keys_ref, bf16[256,576]{1,0:T(8,128)(2,1)S(1)} %join.7.sums_ref, bf16[1,1024,576]{2,1,0:T(8,128)(2,1)S(1)} %turn.3.refs_0_, bf16[1,1024,576]{2,1,0:T(8,128)(2,1)S(1)} %turn.4.refs_1_, ...), custom_call_target="tpu_custom_call" | custom-call | tf_op jit(solution)/shard_map/attend/pallas_call | solution.py:230
  (3 shorter events, 0.1 us)
Async XLA Ops:
  0.0 7.2 %collective-permute-start = (bf16[1,64,576]{2,1,0:T(8,128)(2,1)}, bf16[1,64,576]{2,1,0:T(8,128)(2,1)S(1)}, u32[]{:S(2)}, u32[]{:S(2)}) collective-permute-start(bf16[1,64,576]{2,1,0:T(8,128)(2,1)} %bitcast.5), channel_id=1, source_target_pairs={{0,8},{1,5},{2,10},{3,7},{4,12},{5,1},{6,14},{7,3},{8,0},{9,13},{1... | collective-permute-start | bytes 221192 | tf_op jit(solution)/shard_map/ppermute | solution.py:85
  4.1 2.3 %copy-start = (bf16[1024,4,576]{0,2,1:T(8,128)(2,1)S(1)}, bf16[1024,4,576]{0,2,1:T(8,128)(2,1)}, u32[]{:S(2)}) copy-start(bf16[1024,4,576]{0,2,1:T(8,128)(2,1)} %param.4) | copy-start | bytes 14155780
  6.4 0.9 %copy-start.1 = (bf16[64,576]{1,0:T(8,128)(2,1)S(1)}, bf16[64,576]{1,0:T(8,128)(2,1)}, u32[]{:S(2)}) copy-start(bf16[64,576]{1,0:T(8,128)(2,1)} %param.5) | copy-start | bytes 221188
  7.3 5.4 %collective-permute-start.1 = (bf16[2,64,576]{2,1,0:T(8,128)(2,1)S(1)}, bf16[2,64,576]{2,1,0:T(8,128)(2,1)S(1)}, u32[]{:S(2)}, u32[]{:S(2)}) collective-permute-start(bf16[2,64,576]{2,1,0:T(8,128)(2,1)S(1)} %join.4.first_ref), channel_id=1, source_target_pairs={{0,2},{1,9},{2,0},{3,11},{4,6},{5,13},{6,4},{7,15},{8,10},{9,1},{1... | collective-permute-start | bytes 442376 | tf_op jit(solution)/shard_map/ppermute | solution.py:85
  12.7 9.4 %copy-start.3 = (s32[4]{0:T(128)S(1)}, s32[4]{0:T(128)}, u32[]{:S(2)}) copy-start(s32[4]{0:T(128)} %start_ref.1) | copy-start | bytes 52
  12.7 7.1 %collective-permute-start.2 = (bf16[4,64,576]{2,1,0:T(8,128)(2,1)S(1)}, bf16[4,64,576]{2,1,0:T(8,128)(2,1)S(1)}, u32[]{:S(2)}, u32[]{:S(2)}) collective-permute-start(bf16[4,64,576]{2,1,0:T(8,128)(2,1)S(1)} %join.5.first_ref), channel_id=1, source_target_pairs={{0,4},{1,3},{2,6},{3,1},{4,0},{5,7},{6,2},{7,5},{8,12},{9,11},{10,... | collective-permute-start | bytes 884744 | tf_op jit(solution)/shard_map/ppermute | solution.py:85
  15.9 13.2 %copy-start.2 = (s32[4,4,8]{2,1,0:T(4,128)S(1)}, s32[4,4,8]{2,1,0:T(4,128)}, u32[]{:S(2)}) copy-start(s32[4,4,8]{2,1,0:T(4,128)} %mask_ref.1) | copy-start | bytes 1540
  19.9 2.2 %collective-permute-start.3 = (bf16[8,64,576]{2,1,0:T(8,128)(2,1)S(1)}, bf16[8,64,576]{2,1,0:T(8,128)(2,1)S(1)}, u32[]{:S(2)}, u32[]{:S(2)}) collective-permute-start(bf16[8,64,576]{2,1,0:T(8,128)(2,1)S(1)} %join.6.held_ref), channel_id=1, source_target_pairs={{0,1},{1,0},{2,3},{3,2},{4,5},{5,4},{6,7},{7,6},{8,9},{9,8},{10,11... | collective-permute-start | bytes 1769480 | tf_op jit(solution)/shard_map/ppermute | solution.py:93
  22.8 6.3 %collective-permute-start.4 = (bf16[128,576]{1,0:T(8,128)(2,1)S(1)}, bf16[128,576]{1,0:T(8,128)(2,1)S(1)}, u32[]{:S(2)}, u32[]{:S(2)}) collective-permute-start(bf16[128,576]{1,0:T(8,128)(2,1)S(1)} %get-tuple-element.17.first_ref), channel_id=1, source_target_pairs={{0,16},{16,0},{1,17},{17,1},{2,18},{18,2},{3,19},{19,3},{4,20},{20... | collective-permute-start | bytes 442376 | tf_op jit(solution)/shard_map/ppermute | solution.py:227

commit v3 on v2

--- a/solution.py
+++ b/solution.py
@@ -113,84 +113,175 @@
         ]
 
 
-def attend_kernel(dims, mask_ref, keys_ref, sums_ref, *refs):
+def widths(most):
+    return list(range(TILE, most, TILE)) + [most]
+
+
+def queries_at(q_refs, at):
+    return jnp.concatenate([q[h, at, :] for q in q_refs for h in range(q.shape[0])], axis=0)
+
+
+def block_at(i, block):
+    return pl.ds(pl.multiple_of(i * block, block), block)
+
+
+def scores_of(q, keys):
+    return score_scale * lax.dot_general(
+        q, keys, (((1,), (1,)), ((), ())), preferred_element_type=jnp.float32
+    )
+
+
+def values_of(weights, keys):
+    return lax.dot_general(
+        weights.astype(jnp.bfloat16),
+        keys,
+        (((1,), (0,)), ((), ())),
+        preferred_element_type=jnp.float32,
+    )
+
+
+def score_kernel(dims, mask_ref, keys_ref, own_ref, *refs):
     heads, cpg, cands, length, block, summ, lat = dims
-    q_refs, (out_ref, near, staged, sem) = refs[:-4], refs[-4:]
+    q_refs, (scores_ref, most_ref, near_ref) = refs[:-3], refs[-3:]
+    group = lax.axis_index("seq")
+    rows = heads * block
+
+    def step(i, _):
+        member, b = i // NBLK, lax.rem(i, NBLK)
+        cand = group * cpg + member
+        near_ref[i, 0:block, :] = keys_ref[block_at(i, block), :]
+        n = jnp.int32(block)
+        for j in range(NBLK - 1):
+            seen = jnp.logical_and(j < b, mask_ref[cand, b, j] == 1)
+
+            @pl.when(seen)
+            def _():
+                near_ref[i, pl.ds(pl.multiple_of(n, summ), block), :] = keys_ref[
+                    pl.ds(pl.multiple_of(member * length + j * block, block), block), :
+                ]
+
+            n = n + jnp.where(seen, block, 0)
+        for d in range(cpg):
+            seen = mask_ref[cand, b, NBLK + group * cpg + d] == 1
+
+            @pl.when(seen)
+            def _():
+                near_ref[i, pl.ds(pl.multiple_of(n, summ), summ), :] = own_ref[
+                    d * summ : (d + 1) * summ, :
+                ]
+
+            n = n + jnp.where(seen, summ, 0)
+        near_ref[i, pl.ds(pl.multiple_of(n, summ), TILE), :] = jnp.zeros(
+            (TILE, near_ref.shape[2]), near_ref.dtype
+        )
+
+        def score(total):
+            scores = scores_of(queries_at(q_refs, block_at(i, block)), near_ref[i, :total, :])
+            pos = lax.rem(lax.broadcasted_iota(jnp.int32, (rows, 1), 0), block)
+            col = lax.broadcasted_iota(jnp.int32, (1, total), 1)
+            least = jnp.where(col < block, col, jnp.where(col < n, -1, block))
+            scores = jnp.where(least <= pos, scores, neg_big)
+            scores_ref[i, :, :total] = scores
+            most_ref[i] = jnp.max(scores, axis=1, keepdims=True)
+
+        low = 0
+        for total in widths(scores_ref.shape[2]):
+            pl.when(jnp.logical_and(n > low, n <= total))(functools.partial(score, total))
+            low = total
+        return 0
+
+    lax.fori_loop(0, cpg * NBLK, step, 0)
+
+
+def finish_kernel(dims, mask_ref, sums_ref, scores_ref, most_ref, near_ref, *refs):
+    heads, cpg, cands, length, block, summ, lat = dims
+    q_refs, (out_ref, far, total_ref, part_ref, staged, sem) = refs[:-6], refs[-6:]
     group = lax.axis_index("seq")
     steps = cpg * NBLK
-    near[...] = jnp.zeros_like(near)
+    far[...] = jnp.zeros_like(far)
+    total_ref[...] = jnp.zeros_like(total_ref)
+    part_ref[...] = jnp.zeros_like(part_ref)
 
     def out_copy(i, slot):
         return pltpu.make_async_copy(
             staged.at[slot], out_ref.at[pl.ds(i * block, block)], sem.at[slot]
         )
 
+    def put(slot):
+        result = (total_ref[...] * part_ref[...]).astype(jnp.bfloat16)
+        staged[slot] = jnp.swapaxes(result.reshape(heads, block, lat), 0, 1)
+
     def step(i, _):
-        slot = lax.rem(i, 2)
+        slot = lax.rem(i + 1, 2)
         member, b = i // NBLK, lax.rem(i, NBLK)
         cand = group * cpg + member
-        near[0:block, :] = keys_ref[pl.ds(pl.multiple_of(i * block, block), block), :]
-        n = jnp.int32(block)
+        own_total = jnp.int32(block)
         for j in range(NBLK - 1):
             seen = jnp.logical_and(j < b, mask_ref[cand, b, j] == 1)
-
-            @pl.when(seen)
-            def _():
-                near[pl.ds(pl.multiple_of(n, summ), block), :] = keys_ref[
-                    pl.ds(pl.multiple_of(member * length + j * block, block), block), :
-                ]
-
-            n = n + jnp.where(seen, block, 0)
+            own_total = own_total + jnp.where(seen, block, 0)
+        n = jnp.int32(0)
         for d in range(cands):
             seen = mask_ref[cand, b, NBLK + d] == 1
             row = ((group ^ (d // cpg)) * cpg + d % cpg) * summ
-
-            @pl.when(seen)
+            away = jnp.logical_and(seen, d // cpg != group)
+
+            @pl.when(away)
             def _():
-                near[pl.ds(pl.multiple_of(n, summ), summ), :] = sums_ref[
+                far[pl.ds(pl.multiple_of(n, summ), summ), :] = sums_ref[
                     pl.ds(pl.multiple_of(row, summ), summ), :
                 ]
 
-            n = n + jnp.where(seen, summ, 0)
-        tiles = (n + TILE - 1) // TILE
-
-        @pl.when(i >= 2)
+            n = n + jnp.where(away, summ, 0)
+            own_total = own_total + jnp.where(jnp.logical_and(seen, d // cpg == group), summ, 0)
+
+        @pl.when(i >= 3)
         def _():
-            out_copy(i - 2, slot).wait()
-
-        def attend(tile_total):
-            total = TILE * tile_total
-            rows = heads * block
-            at = pl.ds(pl.multiple_of(i * block, block), block)
-            q = jnp.concatenate(
-                [q_ref[h, at, :] for q_ref in q_refs for h in range(q_ref.shape[0])], axis=0
-            )
-            scores = lax.dot_general(
-                q, near[:total, :], (((1,), (1,)), ((), ())), preferred_element_type=jnp.float32
-            )
-            pos = lax.rem(lax.broadcasted_iota(jnp.int32, (rows, 1), 0), block)
-            col = lax.broadcasted_iota(jnp.int32, (1, total), 1)
-            least = jnp.where(col < block, col, jnp.where(col < n, -1, block))
-            scores = jnp.where(least <= pos, scores * score_scale, neg_big)
-            weights = jnp.exp2(scores - jnp.max(scores, axis=1, keepdims=True))
+            out_copy(i - 3, slot).wait()
+
+        def finish(total, extra):
+            put(slot)
+            scores = scores_ref[i, :, :total]
+            most = most_ref[i]
+            if extra:
+                more = scores_of(queries_at(q_refs, block_at(i, block)), far[:extra, :])
+                col = lax.broadcasted_iota(jnp.int32, (1, extra), 1)
+                more = jnp.where(col < n, more, neg_big)
+                most = jnp.maximum(most, jnp.max(more, axis=1, keepdims=True))
+            weights = jnp.exp2(scores - most)
             weight_sum = jnp.sum(weights, axis=1, keepdims=True)
-            numerator = lax.dot_general(
-                weights.astype(jnp.bfloat16),
-                near[:total, :lat],
-                (((1,), (0,)), ((), ())),
-                preferred_element_type=jnp.float32,
-            )
-            result = (numerator * (1.0 / weight_sum)).astype(jnp.bfloat16)
-            staged[slot] = jnp.swapaxes(result.reshape(heads, block, lat), 0, 1)
-
-        for tile_total in range(1, near.shape[0] // TILE + 1):
-            pl.when(tiles == tile_total)(functools.partial(attend, tile_total))
-        out_copy(i, slot).start()
+            numerator = values_of(weights, near_ref[i, :total, :lat])
+            if extra:
+                weights = jnp.exp2(more - most)
+                weight_sum = weight_sum + jnp.sum(weights, axis=1, keepdims=True)
+                numerator = numerator + values_of(weights, far[:extra, :lat])
+            total_ref[...] = numerator
+            part_ref[...] = 1.0 / weight_sum
+
+        low = 0
+        for total in widths(scores_ref.shape[2]):
+            fits = jnp.logical_and(own_total > low, own_total <= total)
+            low = total
+            below = -1
+            for extra in [0] + (widths(far.shape[0]) if cands > cpg else []):
+                takes = jnp.logical_and(n > below, n <= extra)
+                pl.when(jnp.logical_and(fits, takes))(functools.partial(finish, total, extra))
+                below = extra
+
+        @pl.when(i >= 1)
+        def _():
+            out_copy(i - 1, slot).start()
+
         return 0
 
     lax.fori_loop(0, steps, step, 0)
-    for i in range(max(steps - 2, 0), steps):
-        out_copy(i, i % 2).wait()
+    last = (steps + 1) % 2
+    if steps >= 3:
+        out_copy(steps - 3, last).wait()
+    put(last)
+    out_copy(steps - 1, last).start()
+    if steps >= 2:
+        out_copy(steps - 2, 1 - last).wait()
+    out_copy(steps - 1, last).wait()
 
 
 def shards(queries, keys, block_mask, summary_start):
@@ -202,8 +293,9 @@
     seq_len = row_total // cpg
     block_len = seq_len // NBLK
     summ_len = block_len // 2
-    most = NBLK * block_len + (total_cands - 1) * summ_len
-    most = -(-most // TILE) * TILE
+    steps, rows = cpg * NBLK, head_count * block_len
+    own_most = -(-(NBLK * block_len + (cpg - 1) * summ_len) // 128) * 128
+    far_most = -(-max(total_cands - cpg, 1) * summ_len // 128) * 128
     vmem = pl.BlockSpec(memory_space=pltpu.VMEM)
     smem = pl.BlockSpec(memory_space=pltpu.SMEM)
 
@@ -220,26 +312,46 @@
         compiler_params=grant(4),
         name="order",
     )(summary_start, held, other)
+    dims = (head_count, cpg, total_cands, seq_len, block_len, summ_len, lat_width)
+    scores, most, near = pl.pallas_call(
+        functools.partial(score_kernel, dims),
+        out_shape=[
+            jax.ShapeDtypeStruct((steps, rows, own_most), jnp.float32),
+            jax.ShapeDtypeStruct((steps, rows, 1), jnp.float32),
+            jax.ShapeDtypeStruct((steps, own_most + TILE, key_width), keys.dtype),
+        ],
+        in_specs=[smem, vmem, vmem] + [vmem] * len(by_head),
+        out_specs=[vmem, vmem, vmem],
+        compiler_params=grant(8),
+        cost_estimate=pl.CostEstimate(
+            flops=2 * steps * rows * own_most * key_width, bytes_accessed=0, transcendentals=0
+        ),
+        name="score",
+    )(block_mask, ordered, own, *by_head)
     sums = own
     bit = 1
     while bit < seq_count:
         pairs = [(i, i ^ bit) for i in range(seq_count)]
-        sums = join(sums, lax.ppermute(sums, "seq", pairs))
+        got = lax.ppermute(sums, "seq", pairs)
+        if 2 * bit >= seq_count:
+            got, scores = lax.optimization_barrier((got, scores))
+        sums = join(sums, got)
         bit *= 2
-    dims = (head_count, cpg, total_cands, seq_len, block_len, summ_len, lat_width)
     return pl.pallas_call(
-        functools.partial(attend_kernel, dims),
+        functools.partial(finish_kernel, dims),
         out_shape=jax.ShapeDtypeStruct((row_total, head_count, lat_width), queries.dtype),
-        in_specs=[smem, vmem, vmem] + [vmem] * len(by_head),
+        in_specs=[smem, vmem, vmem, vmem, vmem] + [vmem] * len(by_head),
         out_specs=pl.BlockSpec(memory_space=pl.ANY),
         scratch_shapes=[
-            pltpu.VMEM((most, key_width), keys.dtype),
+            pltpu.VMEM((far_most, key_width), keys.dtype),
+            pltpu.VMEM((rows, lat_width), jnp.float32),
+            pltpu.VMEM((rows, 1), jnp.float32),
             pltpu.VMEM((2, block_len, head_count, lat_width), queries.dtype),
             pltpu.SemaphoreType.DMA((2,)),
         ],
-        compiler_params=grant(24),
-        name="attend",
-    )(block_mask, ordered, sums, *by_head)
+        compiler_params=grant(12),
+        name="finish",
+    )(block_mask, sums, scores, most, near, *by_head)
 
 
 def solution(mesh):

time: 40 us -> 42.2 us (1.055); the launches traced: 39.9 us -> 41.4 us
  Pallas kernels: 14.6 us -> 20.9 us
  waiting for transfers between devices: 13.8 us -> 9.03 us
    pallas_call x1 -> x2, Pallas kernels: 10.8 us -> 17 us  [the longest x1 11.2 us: shards(): pl.pallas_call(functools.partial(finish_kernel, dims), out_shape=jax.Shap...]
    ppermute x1, waiting for transfers between devices: 4.75 us -> 0.01 us  [shards(): got = lax.ppermute(sums, 'seq', pairs)]
  transfers between devices with their start and end apart: 5 -> 5, of which waited for: 4 -> 3; matrix products, arithmetic and copies ran while one was open for 0% -> 0% of each run, Pallas kernels for 8% -> 21%
where the time goes in v3:
time: 42.2 us; the launch traced here: 41.4 us
  Pallas kernels  20.9 us (50%)
  waiting for transfers between devices  9.03 us (21%)
  starting transfers between devices  8.92 us (21%)
  local copies, waits for them, and re-layouts  2.45 us (6%)
    pallas_call x1, Pallas kernels, shards(): pl.pallas_call(functools.partial(finish_kernel, dims), out_shape=jax.Shap...  11.2 us
    ppermute x3, starting transfers between devices, gather_steps(): got = lax.ppermute(held, 'exp', pairs)  7.29 us
    ppermute x3, waiting for transfers between devices, gather_steps(): got = lax.ppermute(held, 'exp', pairs)  6.94 us
    pallas_call x1, Pallas kernels, shards(): pl.pallas_call(functools.partial(score_kernel, dims), out_shape=[jax.Shap...  5.8 us
    pallas_call x3, Pallas kernels, turn(): pl.pallas_call(turn_kernel, out_shape=jax.ShapeDtypeStruct((total, rows,...  3.1 us
    unnamed x8, local copies, waits for them, and re-layouts  2.45 us
    ppermute x1, waiting for transfers between devices, gather_steps(): other = lax.ppermute(held, 'exp', [(i, i ^ 1) for i in range(count)])  2.08 us
    ppermute x1, starting transfers between devices, shards(): got = lax.ppermute(sums, 'seq', pairs)  1.56 us
  transfers between devices with their start and end apart: 5, of which 3 were waited for; matrix products, arithmetic and copies ran while one was open for 0% of the time, Pallas kernels for 21%

profile of v3, /device:TPU:0, one launch (start us, length us, event | category | flops | bytes accessed | tf_op | source)
XLA Modules:
  0.0 41.4 jit_solution(15579826501473780246)
XLA Ops:
  0.0 4.1 %collective-permute-start = (bf16[1,64,576]{2,1,0:T(8,128)(2,1)}, bf16[1,64,576]{2,1,0:T(8,128)(2,1)S(1)}, u32[]{:S(2)}, u32[]{:S(2)}) collective-permute-start(bf16[1,64,576]{2,1,0:T(8,128)(2,1)} %bitcast.5), channel_id=1, source_target_pairs={{0,8},{1,5},{2,10},{3,7},{4,12},{5,1},{6,14},{7,3},{8,0},{9,13},{1... | collective-permute-start | bytes 221192 | tf_op jit(solution)/shard_map/ppermute | solution.py:85
  4.1 0.0 copy-start
  4.1 2.3 %copy-done = bf16[1024,4,576]{0,2,1:T(8,128)(2,1)S(1)} copy-done((bf16[1024,4,576]{0,2,1:T(8,128)(2,1)S(1)}, bf16[1024,4,576]{0,2,1:T(8,128)(2,1)}, u32[]{:S(2)}) %copy-start) | copy-done | bytes 4718616
  6.4 0.8 %turn.3.refs_0_ = bf16[1,1024,576]{2,1,0:T(8,128)(2,1)S(1)} custom-call(bf16[4,576,1024]{2,1,0:T(8,128)(2,1)S(1)} %bitcast.2), custom_call_target="tpu_custom_call" | custom-call | tf_op jit(solution)/shard_map/turn/pallas_call | solution.py:63
  7.2 0.0 collective-permute-done.second_ref
  7.2 0.1 copy-done.1
  7.3 1.6 %collective-permute-start.1 = (bf16[2,64,576]{2,1,0:T(8,128)(2,1)S(1)}, bf16[2,64,576]{2,1,0:T(8,128)(2,1)S(1)}, u32[]{:S(2)}, u32[]{:S(2)}) collective-permute-start(bf16[2,64,576]{2,1,0:T(8,128)(2,1)S(1)} %join.4.first_ref), channel_id=1, source_target_pairs={{0,2},{1,9},{2,0},{3,11},{4,6},{5,13},{6,4},{7,15},{8,10},{9,1},{1... | collective-permute-start | bytes 442376 | tf_op jit(solution)/shard_map/ppermute | solution.py:85
  8.9 0.8 %turn.4.refs_1_ = bf16[1,1024,576]{2,1,0:T(8,128)(2,1)S(1)} custom-call(bf16[4,576,1024]{2,1,0:T(8,128)(2,1)S(1)} %bitcast.3), custom_call_target="tpu_custom_call" | custom-call | tf_op jit(solution)/shard_map/turn/pallas_call | solution.py:63
  9.7 3.0 %collective-permute-done.1.second_ref = bf16[2,64,576]{2,1,0:T(8,128)(2,1)S(1)} collective-permute-done((bf16[2,64,576]{2,1,0:T(8,128)(2,1)S(1)}, bf16[2,64,576]{2,1,0:T(8,128)(2,1)S(1)}, u32[]{:S(2)}, u32[]{:S(2)}) %collective-permute-start.1) | collective-permute-done | bytes 147488 | tf_op jit(solution)/shard_map/ppermute | solution.py:85
  12.7 0.0 copy-start.3
  12.7 1.6 %collective-permute-start.2 = (bf16[4,64,576]{2,1,0:T(8,128)(2,1)S(1)}, bf16[4,64,576]{2,1,0:T(8,128)(2,1)S(1)}, u32[]{:S(2)}, u32[]{:S(2)}) collective-permute-start(bf16[4,64,576]{2,1,0:T(8,128)(2,1)S(1)} %join.5.first_ref), channel_id=1, source_target_pairs={{0,4},{1,3},{2,6},{3,1},{4,0},{5,7},{6,2},{7,5},{8,12},{9,11},{10,... | collective-permute-start | bytes 884744 | tf_op jit(solution)/shard_map/ppermute | solution.py:85
  14.4 1.6 %turn.5.refs_2_ = bf16[2,1024,576]{2,1,0:T(8,128)(2,1)S(1)} custom-call(bf16[4,576,1024]{2,1,0:T(8,128)(2,1)S(1)} %bitcast.4), custom_call_target="tpu_custom_call" | custom-call | tf_op jit(solution)/shard_map/turn/pallas_call | solution.py:63
  15.9 0.0 copy-start.2
  16.0 3.9 %collective-permute-done.2.second_ref = bf16[4,64,576]{2,1,0:T(8,128)(2,1)S(1)} collective-permute-done((bf16[4,64,576]{2,1,0:T(8,128)(2,1)S(1)}, bf16[4,64,576]{2,1,0:T(8,128)(2,1)S(1)}, u32[]{:S(2)}, u32[]{:S(2)}) %collective-permute-start.2) | collective-permute-done | bytes 294944 | tf_op jit(solution)/shard_map/ppermute | solution.py:85
  19.9 0.1 join.6.held_ref
  19.9 0.1 collective-permute-start.3
  20.0 2.1 %collective-permute-done.3.other_ref = bf16[8,64,576]{2,1,0:T(8,128)(2,1)S(1)} collective-permute-done((bf16[8,64,576]{2,1,0:T(8,128)(2,1)S(1)}, bf16[8,64,576]{2,1,0:T(8,128)(2,1)S(1)}, u32[]{:S(2)}, u32[]{:S(2)}) %collective-permute-start.3) | collective-permute-done | bytes 589856 | tf_op jit(solution)/shard_map/ppermute | solution.py:93
  22.1 0.0 copy-done.3
  22.1 0.7 %order.1 = (bf16[1024,576]{1,0:T(8,128)(2,1)S(1)}, bf16[128,576]{1,0:T(8,128)(2,1)S(1)}) custom-call(s32[4]{0:T(128)S(1)} %copy-done.3, bf16[8,64,576]{2,1,0:T(8,128)(2,1)S(1)} %join.6.held_ref, bf16[8,64,576]{2,1,0:T(8,128)(2,1)S(1)} %collective-permute-done.3.other_ref), custom_call_target="tpu_custom_call" | custom-call | tf_op jit(solution)/shard_map/order/pallas_call | solution.py:304
  22.8 1.6 %collective-permute-start.4 = (bf16[128,576]{1,0:T(8,128)(2,1)S(1)}, bf16[128,576]{1,0:T(8,128)(2,1)S(1)}, u32[]{:S(2)}, u32[]{:S(2)}) collective-permute-start(bf16[128,576]{1,0:T(8,128)(2,1)S(1)} %get-tuple-element.21.own_ref.first_ref), channel_id=1, source_target_pairs={{0,16},{16,0},{1,17},{17,1},{2,18},{18,2},{3,19},{19,3},{4,20},{20... | collective-permute-start | bytes 442376 | tf_op jit(solution)/shard_map/ppermute | solution.py:335
  24.3 0.0 copy-done.2
  24.3 5.8 %score.1 = (f32[8,512,640]{2,1,0:T(8,128)S(1)}, f32[8,512,1]{2,1,0:T(8,128)S(1)}, bf16[8,896,576]{2,1,0:T(8,128)(2,1)S(1)}) custom-call(s32[4,4,8]{2,1,0:T(4,128)S(1)} %copy-done.2, bf16[1024,576]{1,0:T(8,128)(2,1)S(1)} %get-tuple-element.22.keys_ref, bf16[128,576]{1,0:T(8,128)(2,1)S(1)} %get-tuple-element.21.own_ref.first_ref, ...), custom_call_target="tpu_custom_call" | custom-call | flops 3019898880 | tf_op jit(solution)/shard_map/score/pallas_call | solution.py:316
  30.1 0.0 collective-permute-done.4.second_ref
  30.2 11.2 %finish.1 = bf16[1024,4,512]{2,1,0:T(4,128)(2,1)} custom-call(s32[4,4,8]{2,1,0:T(4,128)S(1)} %copy-done.2, bf16[256,576]{1,0:T(8,128)(2,1)S(1)} %join.7.sums_ref, f32[8,512,640]{2,1,0:T(8,128)S(1)} %get-tuple-element.28.scores_ref, f32[8,512,1]{2,1,0:T(8,128)S(1)} %get-tuple-element.29.most_ref, bf16[8,896,576]{2,1,0:T(8,128)(2,1)S(1)} %get-tuple-element.30.near_ref, ...), custom_call_target="tpu_custom_call" | custom-call | tf_op jit(solution)/shard_map/finish/pallas_call | solution.py:340
  (4 shorter events, 0.1 us)
Async XLA Ops:
  0.0 7.2 %collective-permute-start = (bf16[1,64,576]{2,1,0:T(8,128)(2,1)}, bf16[1,64,576]{2,1,0:T(8,128)(2,1)S(1)}, u32[]{:S(2)}, u32[]{:S(2)}) collective-permute-start(bf16[1,64,576]{2,1,0:T(8,128)(2,1)} %bitcast.5), channel_id=1, source_target_pairs={{0,8},{1,5},{2,10},{3,7},{4,12},{5,1},{6,14},{7,3},{8,0},{9,13},{1... | collective-permute-start | bytes 221192 | tf_op jit(solution)/shard_map/ppermute | solution.py:85
  4.1 2.3 %copy-start = (bf16[1024,4,576]{0,2,1:T(8,128)(2,1)S(1)}, bf16[1024,4,576]{0,2,1:T(8,128)(2,1)}, u32[]{:S(2)}) copy-start(bf16[1024,4,576]{0,2,1:T(8,128)(2,1)} %param.4) | copy-start | bytes 14155780
  6.4 0.9 %copy-start.1 = (bf16[64,576]{1,0:T(8,128)(2,1)S(1)}, bf16[64,576]{1,0:T(8,128)(2,1)}, u32[]{:S(2)}) copy-start(bf16[64,576]{1,0:T(8,128)(2,1)} %param.5) | copy-start | bytes 221188
  7.3 5.4 %collective-permute-start.1 = (bf16[2,64,576]{2,1,0:T(8,128)(2,1)S(1)}, bf16[2,64,576]{2,1,0:T(8,128)(2,1)S(1)}, u32[]{:S(2)}, u32[]{:S(2)}) collective-permute-start(bf16[2,64,576]{2,1,0:T(8,128)(2,1)S(1)} %join.4.first_ref), channel_id=1, source_target_pairs={{0,2},{1,9},{2,0},{3,11},{4,6},{5,13},{6,4},{7,15},{8,10},{9,1},{1... | collective-permute-start | bytes 442376 | tf_op jit(solution)/shard_map/ppermute | solution.py:85
  12.7 9.4 %copy-start.3 = (s32[4]{0:T(128)S(1)}, s32[4]{0:T(128)}, u32[]{:S(2)}) copy-start(s32[4]{0:T(128)} %start_ref.1) | copy-start | bytes 52
  12.7 7.1 %collective-permute-start.2 = (bf16[4,64,576]{2,1,0:T(8,128)(2,1)S(1)}, bf16[4,64,576]{2,1,0:T(8,128)(2,1)S(1)}, u32[]{:S(2)}, u32[]{:S(2)}) collective-permute-start(bf16[4,64,576]{2,1,0:T(8,128)(2,1)S(1)} %join.5.first_ref), channel_id=1, source_target_pairs={{0,4},{1,3},{2,6},{3,1},{4,0},{5,7},{6,2},{7,5},{8,12},{9,11},{10,... | collective-permute-start | bytes 884744 | tf_op jit(solution)/shard_map/ppermute | solution.py:85
  15.9 8.4 %copy-start.2 = (s32[4,4,8]{2,1,0:T(4,128)S(1)}, s32[4,4,8]{2,1,0:T(4,128)}, u32[]{:S(2)}) copy-start(s32[4,4,8]{2,1,0:T(4,128)} %mask_ref.3) | copy-start | bytes 1540
  19.9 2.2 %collective-permute-start.3 = (bf16[8,64,576]{2,1,0:T(8,128)(2,1)S(1)}, bf16[8,64,576]{2,1,0:T(8,128)(2,1)S(1)}, u32[]{:S(2)}, u32[]{:S(2)}) collective-permute-start(bf16[8,64,576]{2,1,0:T(8,128)(2,1)S(1)} %join.6.held_ref), channel_id=1, source_target_pairs={{0,1},{1,0},{2,3},{3,2},{4,5},{5,4},{6,7},{7,6},{8,9},{9,8},{10,11... | collective-permute-start | bytes 1769480 | tf_op jit(solution)/shard_map/ppermute | solution.py:93
  22.8 7.4 %collective-permute-start.4 = (bf16[128,576]{1,0:T(8,128)(2,1)S(1)}, bf16[128,576]{1,0:T(8,128)(2,1)S(1)}, u32[]{:S(2)}, u32[]{:S(2)}) collective-permute-start(bf16[128,576]{1,0:T(8,128)(2,1)S(1)} %get-tuple-element.21.own_ref.first_ref), channel_id=1, source_target_pairs={{0,16},{16,0},{1,17},{17,1},{2,18},{18,2},{3,19},{19,3},{4,20},{20... | collective-permute-start | bytes 442376 | tf_op jit(solution)/shard_map/ppermute | solution.py:335

commit v4 on v2

--- a/solution.py
+++ b/solution.py
@@ -115,29 +115,35 @@
 
 def attend_kernel(dims, mask_ref, keys_ref, sums_ref, *refs):
     heads, cpg, cands, length, block, summ, lat = dims
-    q_refs, (out_ref, near, staged, sem) = refs[:-4], refs[-4:]
+    q_refs, (out_ref, near, total_ref, part_ref, staged, sem) = refs[:-6], refs[-6:]
     group = lax.axis_index("seq")
-    steps = cpg * NBLK
+    rows = heads * block
     near[...] = jnp.zeros_like(near)
 
-    def out_copy(i, slot):
+    def out_copy(b, member, slot):
+        at = pl.ds(pl.multiple_of(member * length + b * block, block), block)
         return pltpu.make_async_copy(
-            staged.at[slot], out_ref.at[pl.ds(i * block, block)], sem.at[slot]
+            staged.at[slot, member], out_ref.at[at], sem.at[slot, member]
         )
 
-    def step(i, _):
-        slot = lax.rem(i, 2)
-        member, b = i // NBLK, lax.rem(i, NBLK)
+    def put(slot):
+        for member in range(cpg):
+            result = (total_ref[member] * part_ref[member]).astype(jnp.bfloat16)
+            staged[slot, member] = jnp.swapaxes(result.reshape(heads, block, lat), 0, 1)
+
+    def gather_seen(b, member):
         cand = group * cpg + member
-        near[0:block, :] = keys_ref[pl.ds(pl.multiple_of(i * block, block), block), :]
+        near[member, 0:block, :] = keys_ref[
+            pl.ds(pl.multiple_of(member * length + b * block, block), block), :
+        ]
         n = jnp.int32(block)
         for j in range(NBLK - 1):
             seen = jnp.logical_and(j < b, mask_ref[cand, b, j] == 1)
 
             @pl.when(seen)
             def _():
-                near[pl.ds(pl.multiple_of(n, summ), block), :] = keys_ref[
-                    pl.ds(pl.multiple_of(member * length + j * block, block), block), :
+                near[member, pl.ds(pl.multiple_of(n, summ), block), :] = keys_ref[
+                    member * length + j * block : member * length + (j + 1) * block, :
                 ]
 
             n = n + jnp.where(seen, block, 0)
@@ -147,50 +153,79 @@
 
             @pl.when(seen)
             def _():
-                near[pl.ds(pl.multiple_of(n, summ), summ), :] = sums_ref[
+                near[member, pl.ds(pl.multiple_of(n, summ), summ), :] = sums_ref[
                     pl.ds(pl.multiple_of(row, summ), summ), :
                 ]
 
             n = n + jnp.where(seen, summ, 0)
-        tiles = (n + TILE - 1) // TILE
-
-        @pl.when(i >= 2)
+        return n
+
+    def step(b, _):
+        slot = lax.rem(b + 1, 2)
+        counts = [gather_seen(b, member) for member in range(cpg)]
+        tiles = (functools.reduce(jnp.maximum, counts) + TILE - 1) // TILE
+
+        @pl.when(b >= 3)
         def _():
-            out_copy(i - 2, slot).wait()
+            for member in range(cpg):
+                out_copy(b - 3, member, slot).wait()
 
         def attend(tile_total):
             total = TILE * tile_total
-            rows = heads * block
-            at = pl.ds(pl.multiple_of(i * block, block), block)
-            q = jnp.concatenate(
-                [q_ref[h, at, :] for q_ref in q_refs for h in range(q_ref.shape[0])], axis=0
-            )
-            scores = lax.dot_general(
-                q, near[:total, :], (((1,), (1,)), ((), ())), preferred_element_type=jnp.float32
-            )
-            pos = lax.rem(lax.broadcasted_iota(jnp.int32, (rows, 1), 0), block)
-            col = lax.broadcasted_iota(jnp.int32, (1, total), 1)
-            least = jnp.where(col < block, col, jnp.where(col < n, -1, block))
-            scores = jnp.where(least <= pos, scores * score_scale, neg_big)
-            weights = jnp.exp2(scores - jnp.max(scores, axis=1, keepdims=True))
-            weight_sum = jnp.sum(weights, axis=1, keepdims=True)
-            numerator = lax.dot_general(
-                weights.astype(jnp.bfloat16),
-                near[:total, :lat],
-                (((1,), (0,)), ((), ())),
-                preferred_element_type=jnp.float32,
-            )
-            result = (numerator * (1.0 / weight_sum)).astype(jnp.bfloat16)
-            staged[slot] = jnp.swapaxes(result.reshape(heads, block, lat), 0, 1)
-
-        for tile_total in range(1, near.shape[0] // TILE + 1):
+            put(slot)
+            all_scores = []
+            for member in range(cpg):
+                at = pl.ds(pl.multiple_of(member * length + b * block, block), block)
+                q = jnp.concatenate(
+                    [q_ref[h, at, :] for q_ref in q_refs for h in range(q_ref.shape[0])], axis=0
+                )
+                all_scores.append(
+                    lax.dot_general(
+                        q,
+                        near[member, :total, :],
+                        (((1,), (1,)), ((), ())),
+                        preferred_element_type=jnp.float32,
+                    )
+                )
+            pos = lax.rem(lax.broadcasted_iota(jnp.int32, (rows, block), 0), block)
+            causal = lax.broadcasted_iota(jnp.int32, (rows, block), 1) <= pos
+            col = lax.broadcasted_iota(jnp.int32, (1, total - block), 1) + block
+            for member, scores in enumerate(all_scores):
+                bias = jnp.where(col < counts[member], 0.0, neg_big)
+                first = jnp.where(causal, scores[:, :block] * score_scale, neg_big)
+                rest = scores[:, block:] * score_scale + bias
+                most = jnp.maximum(
+                    jnp.max(first, axis=1, keepdims=True), jnp.max(rest, axis=1, keepdims=True)
+                )
+                weights = jnp.exp2(jnp.concatenate([first, rest], axis=1) - most)
+                part_ref[member] = 1.0 / jnp.sum(weights, axis=1, keepdims=True)
+                total_ref[member] = lax.dot_general(
+                    weights.astype(jnp.bfloat16),
+                    near[member, :total, :lat],
+                    (((1,), (0,)), ((), ())),
+                    preferred_element_type=jnp.float32,
+                )
+
+        for tile_total in range(1, near.shape[1] // TILE + 1):
             pl.when(tiles == tile_total)(functools.partial(attend, tile_total))
-        out_copy(i, slot).start()
+
+        @pl.when(b >= 1)
+        def _():
+            for member in range(cpg):
+                out_copy(b - 1, member, slot).start()
+
         return 0
 
-    lax.fori_loop(0, steps, step, 0)
-    for i in range(max(steps - 2, 0), steps):
-        out_copy(i, i % 2).wait()
+    lax.fori_loop(0, NBLK, step, 0)
+    last = (NBLK + 1) % 2
+    for member in range(cpg):
+        out_copy(NBLK - 3, member, last).wait()
+    put(last)
+    for member in range(cpg):
+        out_copy(NBLK - 1, member, last).start()
+    for member in range(cpg):
+        out_copy(NBLK - 2, member, 1 - last).wait()
+        out_copy(NBLK - 1, member, last).wait()
 
 
 def shards(queries, keys, block_mask, summary_start):
@@ -233,9 +268,11 @@
         in_specs=[smem, vmem, vmem] + [vmem] * len(by_head),
         out_specs=pl.BlockSpec(memory_space=pl.ANY),
         scratch_shapes=[
-            pltpu.VMEM((most, key_width), keys.dtype),
-            pltpu.VMEM((2, block_len, head_count, lat_width), queries.dtype),
-            pltpu.SemaphoreType.DMA((2,)),
+            pltpu.VMEM((cpg, most, key_width), keys.dtype),
+            pltpu.VMEM((cpg, head_count * block_len, lat_width), jnp.float32),
+            pltpu.VMEM((cpg, head_count * block_len, 1), jnp.float32),
+            pltpu.VMEM((2, cpg, block_len, head_count, lat_width), queries.dtype),
+            pltpu.SemaphoreType.DMA((2, cpg)),
         ],
         compiler_params=grant(24),
         name="attend",

time: 40 us -> 39.2 us (0.980)
  the two profiles are of different devices: /device:TPU:0 before, /device:TPU:26 now
where the time goes in v4:
time: 39.2 us; the launch traced here: 39.3 us
  waiting for transfers between devices  19.1 us (49%)
  Pallas kernels  15.1 us (39%)
  starting transfers between devices  2.66 us (7%)
  local copies, waits for them, and re-layouts  2.35 us (6%)
    ppermute x3, waiting for transfers between devices, gather_steps(): got = lax.ppermute(held, 'exp', pairs)  11.3 us
    pallas_call x1, Pallas kernels, shards(): pl.pallas_call(functools.partial(attend_kernel, dims), out_shape=jax.Shap...  11.2 us
    ppermute x1, waiting for transfers between devices, shards(): sums = join(sums, lax.ppermute(sums, 'seq', pairs))  5.71 us
    pallas_call x3, Pallas kernels, turn(): pl.pallas_call(turn_kernel, out_shape=jax.ShapeDtypeStruct((total, rows,...  3.11 us
    unnamed x8, local copies, waits for them, and re-layouts  2.35 us
    ppermute x1, waiting for transfers between devices, gather_steps(): other = lax.ppermute(held, 'exp', [(i, i ^ 1) for i in range(count)])  2.08 us
    ppermute x3, starting transfers between devices, gather_steps(): got = lax.ppermute(held, 'exp', pairs)  1.99 us
  transfers between devices with their start and end apart: 5, of which 5 were waited for; matrix products, arithmetic and copies ran while one was open for 0% of the time, Pallas kernels for 8%

profile of v4, /device:TPU:26, one launch (start us, length us, event | category | flops | bytes accessed | tf_op | source)
XLA Modules:
  0.0 39.3 jit_solution(18193226504417329801)
XLA Ops:
  0.0 0.3 collective-permute-start
  0.3 0.0 copy-start
  0.3 2.3 %copy-done = bf16[1024,4,576]{0,2,1:T(8,128)(2,1)S(1)} copy-done((bf16[1024,4,576]{0,2,1:T(8,128)(2,1)S(1)}, bf16[1024,4,576]{0,2,1:T(8,128)(2,1)}, u32[]{:S(2)}) %copy-start) | copy-done | bytes 4718616
  2.7 0.0 copy-start.1
  2.7 0.8 %turn.3.refs_0_ = bf16[1,1024,576]{2,1,0:T(8,128)(2,1)S(1)} custom-call(bf16[4,576,1024]{2,1,0:T(8,128)(2,1)S(1)} %bitcast.2), custom_call_target="tpu_custom_call" | custom-call | tf_op jit(solution)/shard_map/turn/pallas_call | solution.py:63
  3.5 2.9 %collective-permute-done.second_ref = bf16[1,64,576]{2,1,0:T(8,128)(2,1)S(1)} collective-permute-done((bf16[1,64,576]{2,1,0:T(8,128)(2,1)}, bf16[1,64,576]{2,1,0:T(8,128)(2,1)S(1)}, u32[]{:S(2)}, u32[]{:S(2)}) %collective-permute-start) | collective-permute-done | bytes 73760 | tf_op jit(solution)/shard_map/ppermute | solution.py:85
  6.3 0.0 copy-done.1
  6.3 1.6 %collective-permute-start.1 = (bf16[2,64,576]{2,1,0:T(8,128)(2,1)S(1)}, bf16[2,64,576]{2,1,0:T(8,128)(2,1)S(1)}, u32[]{:S(2)}, u32[]{:S(2)}) collective-permute-start(bf16[2,64,576]{2,1,0:T(8,128)(2,1)S(1)} %join.4.first_ref), channel_id=1, source_target_pairs={{0,2},{1,9},{2,0},{3,11},{4,6},{5,13},{6,4},{7,15},{8,10},{9,1},{1... | collective-permute-start | bytes 442376 | tf_op jit(solution)/shard_map/ppermute | solution.py:85
  7.9 0.8 %turn.4.refs_1_ = bf16[1,1024,576]{2,1,0:T(8,128)(2,1)S(1)} custom-call(bf16[4,576,1024]{2,1,0:T(8,128)(2,1)S(1)} %bitcast.3), custom_call_target="tpu_custom_call" | custom-call | tf_op jit(solution)/shard_map/turn/pallas_call | solution.py:63
  8.7 3.0 %collective-permute-done.1.second_ref = bf16[2,64,576]{2,1,0:T(8,128)(2,1)S(1)} collective-permute-done((bf16[2,64,576]{2,1,0:T(8,128)(2,1)S(1)}, bf16[2,64,576]{2,1,0:T(8,128)(2,1)S(1)}, u32[]{:S(2)}, u32[]{:S(2)}) %collective-permute-start.1) | collective-permute-done | bytes 147488 | tf_op jit(solution)/shard_map/ppermute | solution.py:85
  11.8 0.0 copy-start.3
  11.8 0.1 collective-permute-start.2
  11.8 1.6 %turn.5.refs_2_ = bf16[2,1024,576]{2,1,0:T(8,128)(2,1)S(1)} custom-call(bf16[4,576,1024]{2,1,0:T(8,128)(2,1)S(1)} %bitcast.4), custom_call_target="tpu_custom_call" | custom-call | tf_op jit(solution)/shard_map/turn/pallas_call | solution.py:63
  13.4 0.0 copy-start.2
  13.4 5.5 %collective-permute-done.2.second_ref = bf16[4,64,576]{2,1,0:T(8,128)(2,1)S(1)} collective-permute-done((bf16[4,64,576]{2,1,0:T(8,128)(2,1)S(1)}, bf16[4,64,576]{2,1,0:T(8,128)(2,1)S(1)}, u32[]{:S(2)}, u32[]{:S(2)}) %collective-permute-start.2) | collective-permute-done | bytes 294944 | tf_op jit(solution)/shard_map/ppermute | solution.py:85
  18.9 0.1 join.6.held_ref
  19.0 0.1 collective-permute-start.3
  19.0 2.1 %collective-permute-done.3.other_ref = bf16[8,64,576]{2,1,0:T(8,128)(2,1)S(1)} collective-permute-done((bf16[8,64,576]{2,1,0:T(8,128)(2,1)S(1)}, bf16[8,64,576]{2,1,0:T(8,128)(2,1)S(1)}, u32[]{:S(2)}, u32[]{:S(2)}) %collective-permute-start.3) | collective-permute-done | bytes 589856 | tf_op jit(solution)/shard_map/ppermute | solution.py:93
  21.1 0.0 copy-done.3
  21.1 0.7 %order.1 = (bf16[1024,576]{1,0:T(8,128)(2,1)S(1)}, bf16[128,576]{1,0:T(8,128)(2,1)S(1)}) custom-call(s32[4]{0:T(128)S(1)} %copy-done.3, bf16[8,64,576]{2,1,0:T(8,128)(2,1)S(1)} %join.6.held_ref, bf16[8,64,576]{2,1,0:T(8,128)(2,1)S(1)} %collective-permute-done.3.other_ref), custom_call_target="tpu_custom_call" | custom-call | tf_op jit(solution)/shard_map/order/pallas_call | solution.py:247
  21.8 0.6 %collective-permute-start.4 = (bf16[128,576]{1,0:T(8,128)(2,1)S(1)}, bf16[128,576]{1,0:T(8,128)(2,1)S(1)}, u32[]{:S(2)}, u32[]{:S(2)}) collective-permute-start(bf16[128,576]{1,0:T(8,128)(2,1)S(1)} %get-tuple-element.17.first_ref), channel_id=1, source_target_pairs={{0,16},{16,0},{1,17},{17,1},{2,18},{18,2},{3,19},{19,3},{4,20},{20... | collective-permute-start | bytes 442376 | tf_op jit(solution)/shard_map/ppermute | solution.py:262
  22.4 5.7 %collective-permute-done.4.second_ref = bf16[128,576]{1,0:T(8,128)(2,1)S(1)} collective-permute-done((bf16[128,576]{1,0:T(8,128)(2,1)S(1)}, bf16[128,576]{1,0:T(8,128)(2,1)S(1)}, u32[]{:S(2)}, u32[]{:S(2)}) %collective-permute-start.4) | collective-permute-done | bytes 147488 | tf_op jit(solution)/shard_map/ppermute | solution.py:262
  28.1 0.0 copy-done.2
  28.1 11.2 %attend.1 = bf16[1024,4,512]{2,1,0:T(4,128)(2,1)} custom-call(s32[4,4,8]{2,1,0:T(4,128)S(1)} %copy-done.2, bf16[1024,576]{1,0:T(8,128)(2,1)S(1)} %get-tuple-element.16.keys_ref, bf16[256,576]{1,0:T(8,128)(2,1)S(1)} %join.7.sums_ref, bf16[1,1024,576]{2,1,0:T(8,128)(2,1)S(1)} %turn.3.refs_0_, bf16[1,1024,576]{2,1,0:T(8,128)(2,1)S(1)} %turn.4.refs_1_, ...), custom_call_target="tpu_custom_call" | custom-call | tf_op jit(solution)/shard_map/attend/pallas_call | solution.py:265
  (3 shorter events, 0.1 us)
Async XLA Ops:
  0.0 6.3 %collective-permute-start = (bf16[1,64,576]{2,1,0:T(8,128)(2,1)}, bf16[1,64,576]{2,1,0:T(8,128)(2,1)S(1)}, u32[]{:S(2)}, u32[]{:S(2)}) collective-permute-start(bf16[1,64,576]{2,1,0:T(8,128)(2,1)} %bitcast.5), channel_id=1, source_target_pairs={{0,8},{1,5},{2,10},{3,7},{4,12},{5,1},{6,14},{7,3},{8,0},{9,13},{1... | collective-permute-start | bytes 221192 | tf_op jit(solution)/shard_map/ppermute | solution.py:85
  0.3 2.3 %copy-start = (bf16[1024,4,576]{0,2,1:T(8,128)(2,1)S(1)}, bf16[1024,4,576]{0,2,1:T(8,128)(2,1)}, u32[]{:S(2)}) copy-start(bf16[1024,4,576]{0,2,1:T(8,128)(2,1)} %param.4) | copy-start | bytes 14155780
  2.7 3.6 %copy-start.1 = (bf16[64,576]{1,0:T(8,128)(2,1)S(1)}, bf16[64,576]{1,0:T(8,128)(2,1)}, u32[]{:S(2)}) copy-start(bf16[64,576]{1,0:T(8,128)(2,1)} %param.5) | copy-start | bytes 221188
  6.3 5.4 %collective-permute-start.1 = (bf16[2,64,576]{2,1,0:T(8,128)(2,1)S(1)}, bf16[2,64,576]{2,1,0:T(8,128)(2,1)S(1)}, u32[]{:S(2)}, u32[]{:S(2)}) collective-permute-start(bf16[2,64,576]{2,1,0:T(8,128)(2,1)S(1)} %join.4.first_ref), channel_id=1, source_target_pairs={{0,2},{1,9},{2,0},{3,11},{4,6},{5,13},{6,4},{7,15},{8,10},{9,1},{1... | collective-permute-start | bytes 442376 | tf_op jit(solution)/shard_map/ppermute | solution.py:85
  11.8 9.4 %copy-start.3 = (s32[4]{0:T(128)S(1)}, s32[4]{0:T(128)}, u32[]{:S(2)}) copy-start(s32[4]{0:T(128)} %start_ref.1) | copy-start | bytes 52
  11.8 7.1 %collective-permute-start.2 = (bf16[4,64,576]{2,1,0:T(8,128)(2,1)S(1)}, bf16[4,64,576]{2,1,0:T(8,128)(2,1)S(1)}, u32[]{:S(2)}, u32[]{:S(2)}) collective-permute-start(bf16[4,64,576]{2,1,0:T(8,128)(2,1)S(1)} %join.5.first_ref), channel_id=1, source_target_pairs={{0,4},{1,3},{2,6},{3,1},{4,0},{5,7},{6,2},{7,5},{8,12},{9,11},{10,... | collective-permute-start | bytes 884744 | tf_op jit(solution)/shard_map/ppermute | solution.py:85
  13.4 14.7 %copy-start.2 = (s32[4,4,8]{2,1,0:T(4,128)S(1)}, s32[4,4,8]{2,1,0:T(4,128)}, u32[]{:S(2)}) copy-start(s32[4,4,8]{2,1,0:T(4,128)} %mask_ref.1) | copy-start | bytes 1540
  19.0 2.2 %collective-permute-start.3 = (bf16[8,64,576]{2,1,0:T(8,128)(2,1)S(1)}, bf16[8,64,576]{2,1,0:T(8,128)(2,1)S(1)}, u32[]{:S(2)}, u32[]{:S(2)}) collective-permute-start(bf16[8,64,576]{2,1,0:T(8,128)(2,1)S(1)} %join.6.held_ref), channel_id=1, source_target_pairs={{0,1},{1,0},{2,3},{3,2},{4,5},{5,4},{6,7},{7,6},{8,9},{9,8},{10,11... | collective-permute-start | bytes 1769480 | tf_op jit(solution)/shard_map/ppermute | solution.py:93
  21.8 6.3 %collective-permute-start.4 = (bf16[128,576]{1,0:T(8,128)(2,1)S(1)}, bf16[128,576]{1,0:T(8,128)(2,1)S(1)}, u32[]{:S(2)}, u32[]{:S(2)}) collective-permute-start(bf16[128,576]{1,0:T(8,128)(2,1)S(1)} %get-tuple-element.17.first_ref), channel_id=1, source_target_pairs={{0,16},{16,0},{1,17},{17,1},{2,18},{18,2},{3,19},{19,3},{4,20},{20... | collective-permute-start | bytes 442376 | tf_op jit(solution)/shard_map/ppermute | solution.py:262

commit v5 on v4

--- a/solution.py
+++ b/solution.py
@@ -50,6 +50,22 @@
         compiler_params=grant(2),
         name="join",
     )(first, second)
+
+
+def keep_kernel(in_ref, out_ref):
+    out_ref[...] = in_ref[...]
+
+
+def keep(array):
+    vmem = pl.BlockSpec(memory_space=pltpu.VMEM)
+    return pl.pallas_call(
+        keep_kernel,
+        out_shape=jax.ShapeDtypeStruct(array.shape, array.dtype),
+        in_specs=[vmem],
+        out_specs=vmem,
+        compiler_params=grant(2),
+        name="keep",
+    )(array)
 
 
 def turn_kernel(in_ref, out_ref):
@@ -83,7 +99,9 @@
     for k, (bit_a, bit_b) in enumerate(zip(first, second)):
         pairs = [(i, i ^ (bit_b if i & 1 else bit_a)) for i in range(count)]
         got = lax.ppermute(held, "exp", pairs)
-        due = heads if k == last - 1 else heads * (k + 1) // (last + 1)
+        if k == 0:
+            got, held = lax.optimization_barrier((got, keep(held)))
+        due = heads if k == last - 1 else heads * k // (2 * (last - 1))
         if due > done:
             piece = turn(by_width, done, due - done)
             got, piece = lax.optimization_barrier((got, piece))
@@ -94,9 +112,37 @@
     return held, other, by_head
 
 
-def order_kernel(cpg, offsets_a, offsets_b, start_ref, held_ref, other_ref, keys_ref, own_ref):
+def pick_kernel(cpg, orders, start_ref, held_ref, other_ref, own_ref):
     me = lax.axis_index("exp")
     group = lax.axis_index("seq")
+    shard = held_ref.shape[1]
+    summ = own_ref.shape[0] // cpg
+    length = 2 * held_ref.shape[0] * shard // cpg
+    piece = min(shard, summ)
+    for member in range(cpg):
+        for k in range(summ // piece):
+            row = member * length + start_ref[group * cpg + member] + k * piece
+            owner = row // shard
+            inside = pl.multiple_of(lax.rem(row, shard), piece)
+            slots = [
+                sum(((owner ^ me) // bit % 2) << place for place, bit in enumerate(order))
+                for order in orders
+            ]
+            part = owner % 2
+            slot = jnp.where(part == 0, slots[0], slots[1])
+            at = slice(member * summ + k * piece, member * summ + (k + 1) * piece)
+
+            @pl.when(part == me % 2)
+            def _():
+                own_ref[at, :] = held_ref[slot, pl.ds(inside, piece), :]
+
+            @pl.when(part != me % 2)
+            def _():
+                own_ref[at, :] = other_ref[slot, pl.ds(inside, piece), :]
+
+
+def order_kernel(offsets_a, offsets_b, held_ref, other_ref, keys_ref):
+    me = lax.axis_index("exp")
     part = me % 2
     shard = held_ref.shape[1]
     for s, (a, b) in enumerate(zip(offsets_a, offsets_b)):
@@ -104,21 +150,51 @@
         there = (me ^ 1 ^ jnp.where(part == 0, b, a)) * shard
         keys_ref[pl.ds(pl.multiple_of(here, shard), shard), :] = held_ref[s]
         keys_ref[pl.ds(pl.multiple_of(there, shard), shard), :] = other_ref[s]
-    summ = own_ref.shape[0] // cpg
-    length = keys_ref.shape[0] // cpg
-    for member in range(cpg):
-        row = member * length + start_ref[group * cpg + member]
-        own_ref[member * summ : (member + 1) * summ, :] = keys_ref[
-            pl.ds(pl.multiple_of(row, summ), summ), :
-        ]
-
-
-def attend_kernel(dims, mask_ref, keys_ref, sums_ref, *refs):
+
+
+def prepare_kernel(dims, mask_ref, keys_ref, own_ref, near_ref):
+    heads, cpg, cands, length, block, summ, lat = dims
+    group = lax.axis_index("seq")
+    tail = (cands - cpg) * summ + TILE
+
+    def step(i, _):
+        member, b = i // NBLK, lax.rem(i, NBLK)
+        cand = group * cpg + member
+        near_ref[i, 0:block, :] = keys_ref[pl.ds(pl.multiple_of(i * block, block), block), :]
+        n = jnp.int32(block)
+        for j in range(NBLK - 1):
+            seen = jnp.logical_and(j < b, mask_ref[cand, b, j] == 1)
+
+            @pl.when(seen)
+            def _():
+                near_ref[i, pl.ds(pl.multiple_of(n, summ), block), :] = keys_ref[
+                    pl.ds(pl.multiple_of(member * length + j * block, block), block), :
+                ]
+
+            n = n + jnp.where(seen, block, 0)
+        for d in range(cpg):
+            seen = mask_ref[cand, b, NBLK + group * cpg + d] == 1
+
+            @pl.when(seen)
+            def _():
+                near_ref[i, pl.ds(pl.multiple_of(n, summ), summ), :] = own_ref[
+                    d * summ : (d + 1) * summ, :
+                ]
+
+            n = n + jnp.where(seen, summ, 0)
+        near_ref[i, pl.ds(pl.multiple_of(n, summ), tail), :] = jnp.zeros(
+            (tail, near_ref.shape[2]), near_ref.dtype
+        )
+        return 0
+
+    lax.fori_loop(0, cpg * NBLK, step, 0)
+
+
+def attend_kernel(dims, most, mask_ref, got_ref, sums_ref, *refs):
     heads, cpg, cands, length, block, summ, lat = dims
     q_refs, (out_ref, near, total_ref, part_ref, staged, sem) = refs[:-6], refs[-6:]
     group = lax.axis_index("seq")
     rows = heads * block
-    near[...] = jnp.zeros_like(near)
 
     def out_copy(b, member, slot):
         at = pl.ds(pl.multiple_of(member * length + b * block, block), block)
@@ -131,29 +207,20 @@
             result = (total_ref[member] * part_ref[member]).astype(jnp.bfloat16)
             staged[slot, member] = jnp.swapaxes(result.reshape(heads, block, lat), 0, 1)
 
-    def gather_seen(b, member):
+    def add_seen(b, member):
         cand = group * cpg + member
-        near[member, 0:block, :] = keys_ref[
-            pl.ds(pl.multiple_of(member * length + b * block, block), block), :
-        ]
         n = jnp.int32(block)
         for j in range(NBLK - 1):
-            seen = jnp.logical_and(j < b, mask_ref[cand, b, j] == 1)
+            n = n + jnp.where(jnp.logical_and(j < b, mask_ref[cand, b, j] == 1), block, 0)
+        for d in range(cpg):
+            n = n + jnp.where(mask_ref[cand, b, NBLK + group * cpg + d] == 1, summ, 0)
+        for d in range(cands):
+            seen = jnp.logical_and(mask_ref[cand, b, NBLK + d] == 1, d // cpg != group)
+            row = ((group ^ (d // cpg)) * cpg + d % cpg) * summ
 
             @pl.when(seen)
             def _():
-                near[member, pl.ds(pl.multiple_of(n, summ), block), :] = keys_ref[
-                    member * length + j * block : member * length + (j + 1) * block, :
-                ]
-
-            n = n + jnp.where(seen, block, 0)
-        for d in range(cands):
-            seen = mask_ref[cand, b, NBLK + d] == 1
-            row = ((group ^ (d // cpg)) * cpg + d % cpg) * summ
-
-            @pl.when(seen)
-            def _():
-                near[member, pl.ds(pl.multiple_of(n, summ), summ), :] = sums_ref[
+                near[member * NBLK + b, pl.ds(pl.multiple_of(n, summ), summ), :] = sums_ref[
                     pl.ds(pl.multiple_of(row, summ), summ), :
                 ]
 
@@ -162,7 +229,7 @@
 
     def step(b, _):
         slot = lax.rem(b + 1, 2)
-        counts = [gather_seen(b, member) for member in range(cpg)]
+        counts = [add_seen(b, member) for member in range(cpg)]
         tiles = (functools.reduce(jnp.maximum, counts) + TILE - 1) // TILE
 
         @pl.when(b >= 3)
@@ -182,7 +249,7 @@
                 all_scores.append(
                     lax.dot_general(
                         q,
-                        near[member, :total, :],
+                        near[member * NBLK + b, :total, :],
                         (((1,), (1,)), ((), ())),
                         preferred_element_type=jnp.float32,
                     )
@@ -201,12 +268,12 @@
                 part_ref[member] = 1.0 / jnp.sum(weights, axis=1, keepdims=True)
                 total_ref[member] = lax.dot_general(
                     weights.astype(jnp.bfloat16),
-                    near[member, :total, :lat],
+                    near[member * NBLK + b, :total, :lat],
                     (((1,), (0,)), ((), ())),
                     preferred_element_type=jnp.float32,
                 )
 
-        for tile_total in range(1, near.shape[1] // TILE + 1):
+        for tile_total in range(1, most // TILE + 1):
             pl.when(tiles == tile_total)(functools.partial(attend, tile_total))
 
         @pl.when(b >= 1)
@@ -244,39 +311,62 @@
 
     held, other, by_head = gather_steps(keys, queries)
     first, second = step_orders(lax.axis_size("exp"))
-    ordered, own = pl.pallas_call(
-        functools.partial(order_kernel, cpg, slot_offsets(first), slot_offsets(second)),
-        out_shape=[
-            jax.ShapeDtypeStruct((row_total, key_width), keys.dtype),
-            jax.ShapeDtypeStruct((cpg * summ_len, key_width), keys.dtype),
-        ],
+    own = pl.pallas_call(
+        functools.partial(pick_kernel, cpg, (first, second)),
+        out_shape=jax.ShapeDtypeStruct((cpg * summ_len, key_width), keys.dtype),
         in_specs=[smem, vmem, vmem],
-        out_specs=[vmem, vmem],
-        compiler_params=grant(4),
+        out_specs=vmem,
+        compiler_params=grant(2),
+        name="pick",
+    )(summary_start, held, other)
+    ordered = pl.pallas_call(
+        functools.partial(order_kernel, slot_offsets(first), slot_offsets(second)),
+        out_shape=jax.ShapeDtypeStruct((row_total, key_width), keys.dtype),
+        in_specs=[vmem, vmem],
+        out_specs=vmem,
+        compiler_params=grant(2),
+        cost_estimate=pl.CostEstimate(flops=10**9, bytes_accessed=0, transcendentals=0),
         name="order",
-    )(summary_start, held, other)
+    )(held, other)
+    dims = (head_count, cpg, total_cands, seq_len, block_len, summ_len, lat_width)
+    near_rows = NBLK * block_len + (total_cands - 1) * summ_len + TILE
+    near = pl.pallas_call(
+        functools.partial(prepare_kernel, dims),
+        out_shape=jax.ShapeDtypeStruct((cpg * NBLK, near_rows, key_width), keys.dtype),
+        in_specs=[smem, vmem, vmem],
+        out_specs=vmem,
+        compiler_params=grant(2),
+        cost_estimate=pl.CostEstimate(flops=10**9, bytes_accessed=0, transcendentals=0),
+        name="prepare",
+    )(block_mask, ordered, own)
     sums = own
     bit = 1
     while bit < seq_count:
         pairs = [(i, i ^ bit) for i in range(seq_count)]
-        sums = join(sums, lax.ppermute(sums, "seq", pairs))
+        got = lax.ppermute(sums, "seq", pairs)
+        if 2 * bit >= seq_count:
+            got, near = lax.optimization_barrier((got, near))
+        sums = join(sums, got)
         bit *= 2
-    dims = (head_count, cpg, total_cands, seq_len, block_len, summ_len, lat_width)
+    rows = head_count * block_len
     return pl.pallas_call(
-        functools.partial(attend_kernel, dims),
-        out_shape=jax.ShapeDtypeStruct((row_total, head_count, lat_width), queries.dtype),
+        functools.partial(attend_kernel, dims, most),
+        out_shape=[
+            jax.ShapeDtypeStruct((row_total, head_count, lat_width), queries.dtype),
+            jax.ShapeDtypeStruct(near.shape, near.dtype),
+        ],
         in_specs=[smem, vmem, vmem] + [vmem] * len(by_head),
-        out_specs=pl.BlockSpec(memory_space=pl.ANY),
+        out_specs=[pl.BlockSpec(memory_space=pl.ANY), vmem],
         scratch_shapes=[
-            pltpu.VMEM((cpg, most, key_width), keys.dtype),
-            pltpu.VMEM((cpg, head_count * block_len, lat_width), jnp.float32),
-            pltpu.VMEM((cpg, head_count * block_len, 1), jnp.float32),
+            pltpu.VMEM((cpg, rows, lat_width), jnp.float32),
+            pltpu.VMEM((cpg, rows, 1), jnp.float32),
             pltpu.VMEM((2, cpg, block_len, head_count, lat_width), queries.dtype),
             pltpu.SemaphoreType.DMA((2, cpg)),
         ],
-        compiler_params=grant(24),
+        input_output_aliases={1: 1},
+        compiler_params=grant(20),
         name="attend",
-    )(block_mask, ordered, sums, *by_head)
+    )(block_mask, near, sums, *by_head)[0]
 
 
 def solution(mesh):

time: 39.2 us -> 38.7 us (0.987)
  the two profiles are of different devices: /device:TPU:26 before, /device:TPU:0 now
where the time goes in v5:
time: 38.7 us; the launch traced here: 38.5 us
  Pallas kernels  15.6 us (40%)
  starting transfers between devices  9.99 us (26%)
  waiting for transfers between devices  9.56 us (25%)
  local copies, waits for them, and re-layouts  3.27 us (8%)
    pallas_call x1, Pallas kernels, shards(): pl.pallas_call(functools.partial(attend_kernel, dims, most), out_shape=[j...  9.91 us
    ppermute x3, starting transfers between devices, gather_steps(): got = lax.ppermute(held, 'exp', pairs)  8.04 us
    ppermute x3, waiting for transfers between devices, gather_steps(): got = lax.ppermute(held, 'exp', pairs)  4.78 us
    unnamed x8, local copies, waits for them, and re-layouts  3.27 us
    pallas_call x2, Pallas kernels, turn(): pl.pallas_call(turn_kernel, out_shape=jax.ShapeDtypeStruct((total, rows,...  3.1 us
    ppermute x1, waiting for transfers between devices, shards(): got = lax.ppermute(sums, 'seq', pairs)  2.7 us
    ppermute x1, waiting for transfers between devices, gather_steps(): other = lax.ppermute(held, 'exp', [(i, i ^ 1) for i in range(count)])  2.08 us
    ppermute x1, starting transfers between devices, shards(): got = lax.ppermute(sums, 'seq', pairs)  1.89 us
  transfers between devices with their start and end apart: 5, of which 5 were waited for; matrix products, arithmetic and copies ran while one was open for 0% of the time, Pallas kernels for 13%

profile of v5, /device:TPU:0, one launch (start us, length us, event | category | flops | bytes accessed | tf_op | source)
XLA Modules:
  0.0 38.5 jit_solution(1638792891092237348)
XLA Ops:
  0.0 4.1 %collective-permute-start = (bf16[1,64,576]{2,1,0:T(8,128)(2,1)}, bf16[1,64,576]{2,1,0:T(8,128)(2,1)S(1)}, u32[]{:S(2)}, u32[]{:S(2)}) collective-permute-start(bf16[1,64,576]{2,1,0:T(8,128)(2,1)} %bitcast.4), channel_id=1, source_target_pairs={{0,8},{1,5},{2,10},{3,7},{4,12},{5,1},{6,14},{7,3},{8,0},{9,13},{1... | collective-permute-start | bytes 221192 | tf_op jit(solution)/shard_map/ppermute | solution.py:101
  4.1 0.0 copy-start.1
  4.1 0.9 %copy-done.1 = bf16[64,576]{1,0:T(8,128)(2,1)S(1)} copy-done((bf16[64,576]{1,0:T(8,128)(2,1)S(1)}, bf16[64,576]{1,0:T(8,128)(2,1)}, u32[]{:S(2)}) %copy-start.1) | copy-done | bytes 73752
  5.0 1.7 %collective-permute-done.second_ref = bf16[1,64,576]{2,1,0:T(8,128)(2,1)S(1)} collective-permute-done((bf16[1,64,576]{2,1,0:T(8,128)(2,1)}, bf16[1,64,576]{2,1,0:T(8,128)(2,1)S(1)}, u32[]{:S(2)}, u32[]{:S(2)}) %collective-permute-start) | collective-permute-done | bytes 73760 | tf_op jit(solution)/shard_map/ppermute | solution.py:101
  6.7 1.9 %collective-permute-start.1 = (bf16[2,64,576]{2,1,0:T(8,128)(2,1)S(1)}, bf16[2,64,576]{2,1,0:T(8,128)(2,1)S(1)}, u32[]{:S(2)}, u32[]{:S(2)}) collective-permute-start(bf16[2,64,576]{2,1,0:T(8,128)(2,1)S(1)} %join.4.first_ref), channel_id=1, source_target_pairs={{0,2},{1,9},{2,0},{3,11},{4,6},{5,13},{6,4},{7,15},{8,10},{9,1},{1... | collective-permute-start | bytes 442376 | tf_op jit(solution)/shard_map/ppermute | solution.py:101
  8.6 2.3 %copy-done = bf16[1024,4,576]{0,2,1:T(8,128)(2,1)S(1)} copy-done((bf16[1024,4,576]{0,2,1:T(8,128)(2,1)S(1)}, bf16[1024,4,576]{0,2,1:T(8,128)(2,1)}, u32[]{:S(2)}) %copy-start) | copy-done | bytes 4718616
  11.0 0.8 %turn.2.refs_0_ = bf16[1,1024,576]{2,1,0:T(8,128)(2,1)S(1)} custom-call(bf16[4,576,1024]{2,1,0:T(8,128)(2,1)S(1)} %bitcast.2), custom_call_target="tpu_custom_call" | custom-call | tf_op jit(solution)/shard_map/turn/pallas_call | solution.py:79
  11.7 0.4 collective-permute-done.1.second_ref
  12.1 0.0 copy-start.3
  12.1 2.1 %collective-permute-start.2 = (bf16[4,64,576]{2,1,0:T(8,128)(2,1)S(1)}, bf16[4,64,576]{2,1,0:T(8,128)(2,1)S(1)}, u32[]{:S(2)}, u32[]{:S(2)}) collective-permute-start(bf16[4,64,576]{2,1,0:T(8,128)(2,1)S(1)} %join.5.first_ref), channel_id=1, source_target_pairs={{0,4},{1,3},{2,6},{3,1},{4,0},{5,7},{6,2},{7,5},{8,12},{9,11},{10,... | collective-permute-start | bytes 884744 | tf_op jit(solution)/shard_map/ppermute | solution.py:101
  14.2 2.3 %turn.3.refs_1_ = bf16[3,1024,576]{2,1,0:T(8,128)(2,1)S(1)} custom-call(bf16[4,576,1024]{2,1,0:T(8,128)(2,1)S(1)} %bitcast.3), custom_call_target="tpu_custom_call" | custom-call | tf_op jit(solution)/shard_map/turn/pallas_call | solution.py:79
  16.5 0.0 copy-start.2
  16.5 2.7 %collective-permute-done.2.second_ref = bf16[4,64,576]{2,1,0:T(8,128)(2,1)S(1)} collective-permute-done((bf16[4,64,576]{2,1,0:T(8,128)(2,1)S(1)}, bf16[4,64,576]{2,1,0:T(8,128)(2,1)S(1)}, u32[]{:S(2)}, u32[]{:S(2)}) %collective-permute-start.2) | collective-permute-done | bytes 294944 | tf_op jit(solution)/shard_map/ppermute | solution.py:101
  19.3 0.1 join.6.held_ref
  19.3 0.1 collective-permute-start.3
  19.4 2.1 %collective-permute-done.3.other_ref = bf16[8,64,576]{2,1,0:T(8,128)(2,1)S(1)} collective-permute-done((bf16[8,64,576]{2,1,0:T(8,128)(2,1)S(1)}, bf16[8,64,576]{2,1,0:T(8,128)(2,1)S(1)}, u32[]{:S(2)}, u32[]{:S(2)}) %collective-permute-start.3) | collective-permute-done | bytes 589856 | tf_op jit(solution)/shard_map/ppermute | solution.py:111
  21.5 0.0 copy-done.3
  21.5 0.6 %pick.1.own_ref.first_ref = bf16[128,576]{1,0:T(8,128)(2,1)S(1)} custom-call(s32[4]{0:T(128)S(1)} %copy-done.3, bf16[8,64,576]{2,1,0:T(8,128)(2,1)S(1)} %join.6.held_ref, bf16[8,64,576]{2,1,0:T(8,128)(2,1)S(1)} %collective-permute-done.3.other_ref), custom_call_target="tpu_custom_call" | custom-call | tf_op jit(solution)/shard_map/pick/pallas_call | solution.py:314
  22.2 1.9 %collective-permute-start.4 = (bf16[128,576]{1,0:T(8,128)(2,1)S(1)}, bf16[128,576]{1,0:T(8,128)(2,1)S(1)}, u32[]{:S(2)}, u32[]{:S(2)}) collective-permute-start(bf16[128,576]{1,0:T(8,128)(2,1)S(1)} %pick.1.own_ref.first_ref), channel_id=1, source_target_pairs={{0,16},{16,0},{1,17},{17,1},{2,18},{18,2},{3,19},{19,3},{4,20},{20... | collective-permute-start | bytes 442376 | tf_op jit(solution)/shard_map/ppermute | solution.py:346
  24.0 0.1 order.1.keys_ref
  24.2 0.0 copy-done.2
  24.2 1.7 %prepare.1.got_ref = bf16[8,960,576]{2,1,0:T(8,128)(2,1)S(1)} custom-call(s32[4,4,8]{2,1,0:T(4,128)S(1)} %copy-done.2, bf16[1024,576]{1,0:T(8,128)(2,1)S(1)} %order.1.keys_ref, bf16[128,576]{1,0:T(8,128)(2,1)S(1)} %pick.1.own_ref.first_ref), custom_call_target="tpu_custom_call" | custom-call | flops 1000000000 | tf_op jit(solution)/shard_map/prepare/pallas_call | solution.py:333
  25.9 2.7 %collective-permute-done.4.second_ref = bf16[128,576]{1,0:T(8,128)(2,1)S(1)} collective-permute-done((bf16[128,576]{1,0:T(8,128)(2,1)S(1)}, bf16[128,576]{1,0:T(8,128)(2,1)S(1)}, u32[]{:S(2)}, u32[]{:S(2)}) %collective-permute-start.4) | collective-permute-done | bytes 147488 | tf_op jit(solution)/shard_map/ppermute | solution.py:346
  28.6 9.9 %attend.1 = (bf16[1024,4,512]{2,1,0:T(4,128)(2,1)}, bf16[8,960,576]{2,1,0:T(8,128)(2,1)S(1)}) custom-call(s32[4,4,8]{2,1,0:T(4,128)S(1)} %copy-done.2, bf16[8,960,576]{2,1,0:T(8,128)(2,1)S(1)} %prepare.1.got_ref, bf16[256,576]{1,0:T(8,128)(2,1)S(1)} %join.7.sums_ref, bf16[1,1024,576]{2,1,0:T(8,128)(2,1)S(1)} %turn.2.refs_0_, ...), custom_call_target="tpu_custom_call", output_to_operand_aliasing={{1}: (1, {})} | custom-call | tf_op jit(solution)/shard_map/attend/pallas_call | solution.py:352
  (5 shorter events, 0.1 us)
Async XLA Ops:
  0.0 6.7 %collective-permute-start = (bf16[1,64,576]{2,1,0:T(8,128)(2,1)}, bf16[1,64,576]{2,1,0:T(8,128)(2,1)S(1)}, u32[]{:S(2)}, u32[]{:S(2)}) collective-permute-start(bf16[1,64,576]{2,1,0:T(8,128)(2,1)} %bitcast.4), channel_id=1, source_target_pairs={{0,8},{1,5},{2,10},{3,7},{4,12},{5,1},{6,14},{7,3},{8,0},{9,13},{1... | collective-permute-start | bytes 221192 | tf_op jit(solution)/shard_map/ppermute | solution.py:101
  4.1 0.9 %copy-start.1 = (bf16[64,576]{1,0:T(8,128)(2,1)S(1)}, bf16[64,576]{1,0:T(8,128)(2,1)}, u32[]{:S(2)}) copy-start(bf16[64,576]{1,0:T(8,128)(2,1)} %param.5) | copy-start | bytes 221188
  6.7 5.4 %collective-permute-start.1 = (bf16[2,64,576]{2,1,0:T(8,128)(2,1)S(1)}, bf16[2,64,576]{2,1,0:T(8,128)(2,1)S(1)}, u32[]{:S(2)}, u32[]{:S(2)}) collective-permute-start(bf16[2,64,576]{2,1,0:T(8,128)(2,1)S(1)} %join.4.first_ref), channel_id=1, source_target_pairs={{0,2},{1,9},{2,0},{3,11},{4,6},{5,13},{6,4},{7,15},{8,10},{9,1},{1... | collective-permute-start | bytes 442376 | tf_op jit(solution)/shard_map/ppermute | solution.py:101
  8.6 2.3 %copy-start = (bf16[1024,4,576]{0,2,1:T(8,128)(2,1)S(1)}, bf16[1024,4,576]{0,2,1:T(8,128)(2,1)}, u32[]{:S(2)}) copy-start(bf16[1024,4,576]{0,2,1:T(8,128)(2,1)} %param.4) | copy-start | bytes 14155780
  12.1 9.4 %copy-start.3 = (s32[4]{0:T(128)S(1)}, s32[4]{0:T(128)}, u32[]{:S(2)}) copy-start(s32[4]{0:T(128)} %start_ref.1) | copy-start | bytes 52
  12.1 7.1 %collective-permute-start.2 = (bf16[4,64,576]{2,1,0:T(8,128)(2,1)S(1)}, bf16[4,64,576]{2,1,0:T(8,128)(2,1)S(1)}, u32[]{:S(2)}, u32[]{:S(2)}) collective-permute-start(bf16[4,64,576]{2,1,0:T(8,128)(2,1)S(1)} %join.5.first_ref), channel_id=1, source_target_pairs={{0,4},{1,3},{2,6},{3,1},{4,0},{5,7},{6,2},{7,5},{8,12},{9,11},{10,... | collective-permute-start | bytes 884744 | tf_op jit(solution)/shard_map/ppermute | solution.py:101
  16.5 7.6 %copy-start.2 = (s32[4,4,8]{2,1,0:T(4,128)S(1)}, s32[4,4,8]{2,1,0:T(4,128)}, u32[]{:S(2)}) copy-start(s32[4,4,8]{2,1,0:T(4,128)} %mask_ref.3) | copy-start | bytes 1540
  19.3 2.2 %collective-permute-start.3 = (bf16[8,64,576]{2,1,0:T(8,128)(2,1)S(1)}, bf16[8,64,576]{2,1,0:T(8,128)(2,1)S(1)}, u32[]{:S(2)}, u32[]{:S(2)}) collective-permute-start(bf16[8,64,576]{2,1,0:T(8,128)(2,1)S(1)} %join.6.held_ref), channel_id=1, source_target_pairs={{0,1},{1,0},{2,3},{3,2},{4,5},{5,4},{6,7},{7,6},{8,9},{9,8},{10,11... | collective-permute-start | bytes 1769480 | tf_op jit(solution)/shard_map/ppermute | solution.py:111
  22.2 6.4 %collective-permute-start.4 = (bf16[128,576]{1,0:T(8,128)(2,1)S(1)}, bf16[128,576]{1,0:T(8,128)(2,1)S(1)}, u32[]{:S(2)}, u32[]{:S(2)}) collective-permute-start(bf16[128,576]{1,0:T(8,128)(2,1)S(1)} %pick.1.own_ref.first_ref), channel_id=1, source_target_pairs={{0,16},{16,0},{1,17},{17,1},{2,18},{18,2},{3,19},{19,3},{4,20},{20... | collective-permute-start | bytes 442376 | tf_op jit(solution)/shard_map/ppermute | solution.py:346
